TPU v7x, 128 devices: a whole 4x4x4 slice. The times are simulated.
128 devices in a mesh: exp: 32 (over z, x_lo, y), row: 4 (over x_hi, core).
Axes of the slice: x: 4 (x_hi: 2, x_lo: 2; x = x_hi * 2 + x_lo), y: 4, z: 4, core: 2. Of those that a mesh axis runs over, the one named last changes fastest.
Arguments:
- latent: bfloat16 [4, 1024, 1024], P(None, 'row', 'exp'), may hold values from -6 to 6
- row_taps: bfloat16 [16, 21], replicated, may hold values from -1.25 to 1.25
- column_taps: bfloat16 [16, 21], replicated, may hold values from -1.25 to 1.25
- coefficients: bfloat16 [32, 16, 1024, 1024], P('exp', None, 'row'), may hold values from -1.5 to 1.5
- observed: bfloat16 [32, 1024, 1024], P('exp', 'row'), may hold values from -6 to 6
- cell_of: int32 [32, 1], replicated, may hold values from 0 to 3
- valid_rows: int32 [32, 1024], P('exp', 'row'), may hold values 0 or 1
Outputs:
- gradient: float32 [4, 1024, 1024], P(None, 'row', 'exp')
- residuals: float32 [32, 1024, 1024], P('exp', 'row')
Inputs may be any that keep to these rules, and one draw needn't show every extreme that they name: `cell_of`: every sky cell is covered by at least one exposure.
All inputs are finite; a program needn't handle non-finite values. No bound on the sum of `valid_rows` on one device may be relied on, other than what follows from the above.
Results may differ from a plain program's by a relative error of at most 0.0023.
Values may be sent and summed in bfloat16 or wider, within the bound.
No kernel may reach another device: no remote copies, remote signals or barrier semaphores. Data moves between devices by JAX's collectives and lax.ppermute only.
A program may use at most 128 MiB of HBM per device.

v0:
```python
import jax
import jax.numpy as jnp
from jax import lax
from jax.experimental import pallas as pl
from jax.experimental.pallas import tpu as pltpu
from jax.sharding import PartitionSpec as P


F32 = jnp.float32
BF16 = jnp.bfloat16
KERNELS = 16
PAIRS = KERNELS // 2
TAPS = 21
HALF = TAPS // 2
CELLS = 4
EXPOSURES = 32
ROWS = 256
COLS = 1024
BLOCKS = COLS // 128
OWN = COLS // EXPOSURES
SKY = 24
RIM = 16
LAT = ROWS + 2 * SKY
LATP = 384
EXT = ROWS + 2 * RIM
HOUT = EXT // 2
TOP = 8
RBR = HOUT + 256
WR = 384

VMEM = pl.BlockSpec(memory_space=pltpu.VMEM)
SMEM = pl.BlockSpec(memory_space=pltpu.SMEM)
ANY = pl.BlockSpec(memory_space=pl.ANY)
HBM = pl.BlockSpec(memory_space=pltpu.HBM)


def dot(a, b):
    return lax.dot_general(a, b, (((1,), (0,)), ((), ())), preferred_element_type=F32)


def column_of(valid):
    return jnp.broadcast_to(valid, (128, valid.shape[1])).T


def pack_kernel(even_ref, cell_ref, lat_ref, near_ref, far_ref, out_ref, turned):
    even = even_ref[0, 0] > 0
    fill = jnp.zeros((OWN, LATP - LAT), F32)
    for c in range(CELLS):
        near, far = near_ref[c].astype(F32), far_ref[c].astype(F32)
        above = jnp.where(even, far[:, ROWS - SKY :], near[:, ROWS - SKY :])
        below = jnp.where(even, near[:, :SKY], far[:, :SKY])
        turned[c] = jnp.concatenate([above, lat_ref[c].astype(F32), below, fill], axis=1).astype(BF16)
    for e in range(EXPOSURES):
        out_ref[e] = turned[cell_ref[0, e]]


def pack(even, cell_of, latent, near, far):
    return pl.pallas_call(
        pack_kernel,
        out_shape=jax.ShapeDtypeStruct((EXPOSURES, OWN, LATP), BF16),
        in_specs=[SMEM, SMEM, VMEM, VMEM, VMEM],
        out_specs=VMEM,
        scratch_shapes=[pltpu.VMEM((CELLS, OWN, LATP), BF16)],
        name="pack",
    )(even, cell_of, latent, near, far)


def base_rows(taps, place):
    lane = lax.broadcasted_iota(jnp.int32, (KERNELS, 256), 1)
    out = jnp.zeros((KERNELS, 256), F32)
    for t in range(TAPS):
        out = jnp.where(lane == place(t) % 256, taps[:, t : t + 1], out)
    return out


def skewed(row, count):
    return pltpu.roll(jnp.broadcast_to(row, (count, 256)), 0, 1, stride=1, stride_axis=0)


def bands_kernel(row_ref, col_ref, f_ref, c_hbm, a_hbm, b_hbm, c_ref, a_ref, b_ref, sem):
    c_out = pltpu.make_async_copy(c_ref, c_hbm, sem.at[PAIRS + 1])
    a_out = pltpu.make_async_copy(a_ref, a_hbm, sem.at[PAIRS])
    b_out = [pltpu.make_async_copy(b_ref.at[i], b_hbm.at[i], sem.at[i]) for i in range(PAIRS)]
    rows = row_ref[...].astype(F32)
    cols = col_ref[...].astype(F32)
    f_base = base_rows(rows, lambda t: HALF - t)
    b_base = base_rows(rows, lambda t: t - HALF)
    c_base = base_rows(cols, lambda t: t + 2 * RIM - RIM - HALF)
    a_base = base_rows(cols, lambda t: RIM + HALF - t)
    at = lax.broadcasted_iota(jnp.int32, (256, 256), 0)
    out = lax.broadcasted_iota(jnp.int32, (256, 256), 1)
    near = jnp.abs(at - out) < 128
    for k in range(KERNELS):
        i, q = k // 2, k % 2
        f_ref[i, :, 128 * q : 128 * q + 128] = skewed(f_base[k : k + 1], 256)[:, :128].astype(BF16)
        b = skewed(b_base[k : k + 1], 256)
        b_ref[i, 256 * q : 256 * q + 256, :] = jnp.where(near, b, 0.0).astype(BF16)
        far = jnp.where(near, 0.0, b).astype(BF16)
        b_ref[i, 512 + 128 * q : 576 + 128 * q, :] = far[:64]
        b_ref[i, 576 + 128 * q : 640 + 128 * q, :] = far[192:]
        c_ref[k] = skewed(c_base[k : k + 1], HOUT).astype(BF16)
        a_ref[k] = skewed(a_base[k : k + 1], 128).astype(BF16)
        if q == 1:
            b_out[i].start()
    c_out.start()
    a_out.start()
    for copy in (*b_out, c_out, a_out):
        copy.wait()


def make_bands(row_taps, column_taps):
    return pl.pallas_call(
        bands_kernel,
        out_shape=(
            jax.ShapeDtypeStruct((PAIRS, 256, 256), BF16),
            jax.ShapeDtypeStruct((KERNELS, HOUT, 256), BF16),
            jax.ShapeDtypeStruct((KERNELS, 128, 256), BF16),
            jax.ShapeDtypeStruct((PAIRS, 768, 256), BF16),
        ),
        in_specs=[VMEM, VMEM],
        out_specs=(VMEM, HBM, HBM, HBM),
        scratch_shapes=[
            pltpu.VMEM((KERNELS, HOUT, 256), BF16),
            pltpu.VMEM((KERNELS, 128, 256), BF16),
            pltpu.VMEM((PAIRS, 768, 256), BF16),
            pltpu.SemaphoreType.DMA((PAIRS + 2,)),
        ],
        compiler_params=pltpu.CompilerParams(vmem_limit_bytes=56 << 20),
        name="bands",
    )(row_taps, column_taps)


def main_kernel(
    even_ref, strip_ref, valid_ref, f_hbm, c_hbm, a_hbm, b_hbm, coef_hbm, obs_hbm, near_hbm, far_hbm,
    res_hbm, send_ref,
    f_ref, c_ref, a_ref, b_ref, sky, windows, coef, obs, rb, rb2, pred, w, w2, cb, cb2, acc, sem, rim_sem, band_sem,
):
    def coef_in(k):
        return pltpu.make_async_copy(coef_hbm.at[0, k], coef.at[k, pl.ds(RIM, ROWS), :], sem.at[k])

    even = even_ref[0, 0]
    near_at = pl.ds(pl.multiple_of(even * (RIM + ROWS), RIM), RIM)
    far_at = pl.ds(pl.multiple_of((1 - even) * (RIM + ROWS), RIM), RIM)
    rims_in = [
        pltpu.make_async_copy(obs_hbm.at[0], obs.at[pl.ds(RIM, ROWS), :], rim_sem.at[0]),
        pltpu.make_async_copy(near_hbm.at[KERNELS], obs.at[near_at, :], rim_sem.at[1]),
        pltpu.make_async_copy(far_hbm.at[KERNELS], obs.at[far_at, :], rim_sem.at[2]),
        pltpu.make_async_copy(near_hbm.at[pl.ds(0, KERNELS)], coef.at[:, near_at, :], rim_sem.at[3]),
        pltpu.make_async_copy(far_hbm.at[pl.ds(0, KERNELS)], coef.at[:, far_at, :], rim_sem.at[4]),
    ]
    f_in = pltpu.make_async_copy(f_hbm, f_ref, band_sem.at[3])
    c_in = pltpu.make_async_copy(c_hbm, c_ref, band_sem.at[2])
    a_in = pltpu.make_async_copy(a_hbm, a_ref, band_sem.at[0])
    b_in = pltpu.make_async_copy(b_hbm, b_ref, band_sem.at[1])
    for copy in rims_in[:3]:
        copy.start()
    f_in.start()
    c_in.start()
    for copy in rims_in[3:]:
        copy.start()
    for k in range(KERNELS):
        coef_in(k).start()
    a_in.start()
    b_in.start()

    for r in (rb, rb2):
        r[:, :, 0:TOP, :] = jnp.zeros((2, BLOCKS, TOP, 128), BF16)
        r[:, :, TOP + LAT :, :] = jnp.zeros((2, BLOCKS, RBR - LAT - TOP, 128), BF16)
    for r in (w, w2):
        r[:, :, EXT:, :] = jnp.zeros((2, BLOCKS, WR - EXT, 128), BF16)
    acc[...] = jnp.zeros_like(acc)
    low = lax.broadcasted_iota(jnp.int32, (LAT, 128), 1) < 64
    for j in range(BLOCKS):
        sky[j] = strip_ref[128 * j : 128 * j + 128, :].astype(F32).T[:LAT]
    zero = jnp.zeros((LAT, 128), F32)
    for j in range(BLOCKS):
        after = sky[j + 1] if j + 1 < BLOCKS else zero
        before = sky[j - 1] if j > 0 else zero
        windows[j, :, 0:128] = sky[j].astype(BF16)
        windows[j, :, 128:256] = jnp.where(low, after, before).astype(BF16)
    for copy in rims_in[:3]:
        copy.wait()
    pred[...] = -obs[...].astype(F32)
    for copy in rims_in[3:]:
        copy.wait()
    f_in.wait()
    c_in.wait()

    def blur(i, rb):
        f = f_ref[i]
        for j in range(BLOCKS):
            both = dot(windows[j], f)
            rb[0, j, TOP : TOP + LAT, :] = both[:, :128].astype(BF16)
            rb[1, j, TOP : TOP + LAT, :] = both[:, 128:].astype(BF16)

    def predict(i, rb):
        for q in range(2):
            k = 2 * i + q
            c = c_ref[k]
            for h in range(2):
                out = slice(HOUT * h, HOUT * h + HOUT)
                for x in range(0, BLOCKS, 2):
                    at = slice(HOUT * h, HOUT * h + 256)
                    v = dot(c, jnp.concatenate([rb[q, x, at, :], rb[q, x + 1, at, :]], axis=1))
                    cols = slice(128 * x, 128 * x + 256)
                    pred[out, cols] += coef[k, out, cols].astype(F32) * v

    def forward(n, carry):
        for m in range(4):
            coef_in(4 * n + m).wait()
        blur(2 * n, rb)
        blur(2 * n + 1, rb2)
        predict(2 * n, rb)
        predict(2 * n + 1, rb2)
        return carry

    lax.fori_loop(0, PAIRS // 2, forward, 0)

    mask = column_of(valid_ref[...].astype(F32))
    for j in range(BLOCKS):
        pred[RIM : RIM + ROWS, 128 * j : 128 * j + 128] *= mask
    res_out = pltpu.make_async_copy(pred.at[pl.ds(RIM, ROWS), :], res_hbm.at[0], rim_sem.at[0])
    res_out.start()

    low_y = lax.broadcasted_iota(jnp.int32, (ROWS, 128), 1) < 64
    none = jnp.zeros((ROWS, 128), BF16)

    def weigh(i, w):
        for q in range(2):
            for x in range(BLOCKS):
                cols = slice(128 * x, 128 * x + 128)
                w[q, x, 0:EXT, :] = (coef[2 * i + q, :, cols].astype(F32) * pred[:, cols]).astype(BF16)

    def back(i, w, cb):
        for q in range(2):
            a = a_ref[2 * i + q]
            for h in range(2):
                for x in range(0, BLOCKS, 2):
                    at = slice(128 * h, 128 * h + 256)
                    both = dot(a, jnp.concatenate([w[q, x, at, :], w[q, x + 1, at, :]], axis=1))
                    cb[q, x, 128 * h : 128 * h + 128, :] = both[:, :128].astype(BF16)
                    cb[q, x + 1, 128 * h : 128 * h + 128, :] = both[:, 128:].astype(BF16)
        b = b_ref[i]
        for x in range(0, BLOCKS, 2):
            parts = [cb[0, x], cb[0, x + 1], cb[1, x], cb[1, x + 1]]
            for q in range(2):
                after = cb[q, x + 2] if x + 2 < BLOCKS else none
                before = cb[q, x - 1] if x > 0 else none
                parts.append(jnp.where(low_y, after, before))
            acc[x // 2] += dot(jnp.concatenate(parts, axis=1), b)

    weigh(0, w)
    a_in.wait()
    b_in.wait()

    def adjoint(n, carry):
        weigh(2 * n + 1, w2)
        back(2 * n, w, cb)
        weigh(jnp.minimum(2 * n + 2, PAIRS - 1), w)
        back(2 * n + 1, w2, cb2)
        return carry

    lax.fori_loop(0, PAIRS // 2, adjoint, 0)
    for x in range(BLOCKS // 2):
        send_ref[256 * x : 256 * x + 256, :] = acc[x].T.astype(BF16)
    res_out.wait()


def main(even, strip, valid, bands, coefficients, observed, near, far):
    return pl.pallas_call(
        main_kernel,
        out_shape=(
            jax.ShapeDtypeStruct((1, ROWS, COLS), F32),
            jax.ShapeDtypeStruct((COLS, ROWS), BF16),
        ),
        in_specs=[SMEM] + [VMEM] * 2 + [HBM] * 6 + [VMEM] * 2,
        out_specs=(ANY, VMEM),
        scratch_shapes=[
            pltpu.VMEM((PAIRS, 256, 256), BF16),
            pltpu.VMEM((KERNELS, HOUT, 256), BF16),
            pltpu.VMEM((KERNELS, 128, 256), BF16),
            pltpu.VMEM((PAIRS, 768, 256), BF16),
            pltpu.VMEM((BLOCKS, LAT, 128), F32),
            pltpu.VMEM((BLOCKS, LAT, 256), BF16),
            pltpu.VMEM((KERNELS, EXT, COLS), BF16),
            pltpu.VMEM((EXT, COLS), BF16),
            pltpu.VMEM((2, BLOCKS, RBR, 128), BF16),
            pltpu.VMEM((2, BLOCKS, RBR, 128), BF16),
            pltpu.VMEM((EXT, COLS), F32),
            pltpu.VMEM((2, BLOCKS, WR, 128), BF16),
            pltpu.VMEM((2, BLOCKS, WR, 128), BF16),
            pltpu.VMEM((2, BLOCKS, ROWS, 128), BF16),
            pltpu.VMEM((2, BLOCKS, ROWS, 128), BF16),
            pltpu.VMEM((BLOCKS // 2, ROWS, 256), F32),
            pltpu.SemaphoreType.DMA((KERNELS,)),
            pltpu.SemaphoreType.DMA((5,)),
            pltpu.SemaphoreType.DMA((4,)),
        ],
        compiler_params=pltpu.CompilerParams(vmem_limit_bytes=56 << 20),
        name="main",
    )(even, strip, valid, *bands, coefficients, observed, near, far)


def gather_kernel(cell_ref, terms_ref, out_ref):
    out_ref[...] = jnp.zeros_like(out_ref)
    for e in range(EXPOSURES):
        out_ref[cell_ref[0, e]] += terms_ref[e].astype(F32)


def gather(cell_of, terms):
    return pl.pallas_call(
        gather_kernel,
        out_shape=jax.ShapeDtypeStruct((CELLS, OWN, ROWS), F32),
        in_specs=[SMEM, VMEM],
        out_specs=VMEM,
        name="gather",
    )(cell_of, terms)


def keep(*arrays):
    return [pltpu.with_memory_space_constraint(a, pltpu.VMEM) for a in arrays]


def body(latent, row_taps, column_taps, coefficients, observed, cell_of, valid_rows):
    count = lax.axis_size("row")
    even = 1 - lax.rem(lax.axis_index("row"), 2)
    chip = [(i, i ^ 1) for i in range(count)]
    across = [(i, i + 1) for i in range(1, count - 1, 2)] + [(i + 1, i) for i in range(1, count - 1, 2)]
    cell_of = cell_of.reshape(1, EXPOSURES)
    latent = jnp.swapaxes(latent, 1, 2)

    def rim(start):
        coef = lax.dynamic_slice_in_dim(coefficients[0], start, RIM, 1)
        seen = lax.dynamic_slice_in_dim(observed, start, RIM, 1)
        usable = lax.dynamic_slice_in_dim(valid_rows[0], start, RIM, 0).astype(BF16)
        return jnp.concatenate([coef, seen], axis=0) * usable[None, :, None]

    far_sky = lax.ppermute(latent, "row", across)
    near_sky = lax.ppermute(latent, "row", chip)
    far_rim = rim((1 - even) * (ROWS - RIM))
    near_rim = rim(even * (ROWS - RIM))
    far_rim = lax.ppermute(far_rim, "row", across)
    near_rim = lax.ppermute(near_rim, "row", chip)
    even = even.reshape(1, 1)
    packed = pack(even, cell_of, latent, *keep(near_sky, far_sky))
    strip = lax.all_to_all(packed, "exp", 0, 0, tiled=True)
    f, c, a, b = make_bands(row_taps, column_taps)
    strip = strip.reshape(COLS, LATP)
    residual, send = main(
        even, *keep(strip), valid_rows, (f, c, a, b), coefficients, observed, *keep(near_rim, far_rim)
    )
    terms = lax.all_to_all(send.reshape(EXPOSURES, OWN, ROWS), "exp", 0, 0, tiled=True)
    return jnp.swapaxes(gather(cell_of, *keep(terms)), 1, 2), residual


def solution(mesh):
    placed = (
        P(None, "row", "exp"),
        P(),
        P(),
        P("exp", None, "row", None),
        P("exp", "row", None),
        P(),
        P("exp", "row"),
    )
    return jax.shard_map(
        body,
        mesh=mesh,
        in_specs=placed,
        out_specs=(P(None, "row", "exp"), P("exp", "row", None)),
        check_vma=False,
    )
```

profile of v0, /device:TPU:4, one launch (start us, length us, event | category | flops | bytes accessed | tf_op | source)
XLA Modules:
  0.0 73.2 jit_solution(4124139998366305686)
XLA Ops:
  0.6 1.9 %collective-permute-start.1 = (bf16[4,32,256]{2,1,0:T(8,128)(2,1)}, bf16[4,32,256]{2,1,0:T(8,128)(2,1)S(1)}, u32[]{:S(2)}, u32[]{:S(2)}) collective-permute-start(bf16[4,32,256]{2,1,0:T(8,128)(2,1)} %bitcast.17), channel_id=1, source_target_pairs={{1,2},{2,1},{5,6},{6,5},{9,10},{10,9},{13,14},{14,13},{17,18},{18,... | collective-permute-start | bytes 196616 | tf_op jit(solution)/shard_map/ppermute | solution.py:338
  2.6 0.1 collective-permute-start
  2.7 0.8 %fusion.3 = (bf16[16]{0:T(256)(128)(2,1)S(1)}, bf16[16]{0:T(256)(128)(2,1)S(1)}) fusion(s32[1,256]{1,0:T(1,128)} %valid_ref.1, s32[]{:T(128)S(6)} %select_n.5, s32[]{:T(128)S(6)} %select_n.4), kind=kLoop, calls=%fused_computation.11 | loop fusion | flops 32 | bytes 200 | tf_op jit(solution)/shard_map/convert_element_type | solution.py:335
  3.4 0.8 %constant_dynamic-slice_fusion.1 = (bf16[1,16,1024]{2,1,0:T(8,128)(2,1)S(1)}, bf16[1,16,1024]{2,1,0:T(8,128)(2,1)S(1)}) fusion(bf16[1,256,1024]{2,1,0:T(8,128)(2,1)} %obs_hbm.1, s32[]{:T(128)S(6)} %select_n.5, s32[]{:T(128)S(6)} %select_n.4), kind=kLoop, calls=%fused_computation.5 | loop fusion | bytes 131080 | tf_op jit(solution)/shard_map/dynamic_slice | solution.py:334
  4.2 1.3 %dynamic-slice_bitcast_fusion = (bf16[16,16,1024]{2,1,0:T(8,128)(2,1)S(1)}, bf16[16,16,1024]{2,1,0:T(8,128)(2,1)S(1)}) fusion(bf16[1,16,256,1024]{3,2,1,0:T(8,128)(2,1)} %coef_hbm.1, s32[]{:T(128)S(6)} %select_n.5, s32[]{:T(128)S(6)} %select_n.4), kind=kLoop, calls=%fused_computation.2 | loop fusion | bytes 2097160 | tf_op jit(solution)/shard_map/dynamic_slice | solution.py:333
  5.5 0.1 maximum_multiply_fusion
  5.6 0.6 collective-permute-start.2
  6.2 1.8 %collective-permute-done.1.far_ref = bf16[4,32,256]{2,1,0:T(8,128)(2,1)S(1)} collective-permute-done((bf16[4,32,256]{2,1,0:T(8,128)(2,1)}, bf16[4,32,256]{2,1,0:T(8,128)(2,1)S(1)}, u32[]{:S(2)}, u32[]{:S(2)}) %collective-permute-start.1) | collective-permute-done | bytes 65568 | tf_op jit(solution)/shard_map/ppermute | solution.py:338
  7.9 0.0 collective-permute-done.near_ref
  7.9 1.9 %pack.1 = bf16[32,32,384]{2,1,0:T(8,128)(2,1)} custom-call(s32[1,1]{1,0:T(1,128)} %bitcast.1.even_ref, s32[1,32]{1,0:T(1,128)} %bitcast.20, bf16[4,32,256]{2,1,0:T(8,128)(2,1)} %bitcast.19, bf16[4,32,256]{2,1,0:T(8,128)(2,1)S(1)} %collective-permute-done.near_ref, bf16[4,32,256]{2,1,0:T(8,128)(2,1)S(1)} %collective-permute-done.1.far_ref), custom_call_target="tpu_custom_call" | custom-call | tf_op jit(solution)/shard_map/pack/pallas_call | solution.py:58
  9.8 9.0 %all-to-all-start = ((bf16[32,32,384]{2,1,0:T(8,128)(2,1)}), bf16[32,32,384]{2,1,0:T(8,128)(2,1)S(1)}, u32[]{:S(2)}, u32[]{:S(2)}) async-start(bf16[32,32,384]{2,1,0:T(8,128)(2,1)} %pack.1), calls=%async_computation | async-start | bytes 1572864 | tf_op jit(solution)/shard_map/all_to_all | solution.py:346
  18.8 0.1 maximum_multiply_fusion.1
  18.9 2.5 %collective-permute-start.3 = (bf16[17,16,1024]{2,1,0:T(8,128)(2,1)S(1)}, bf16[17,16,1024]{2,1,0:T(8,128)(2,1)S(1)}, u32[]{:S(2)}, u32[]{:S(2)}) collective-permute-start(bf16[17,16,1024]{2,1,0:T(8,128)(2,1)S(1)} %maximum_multiply_fusion.1), channel_id=1, source_target_pairs={{1,2},{2,1},{5,6},{6,5},{9,10},{10,9},{13,14},{14,13},{17,18},{18,... | collective-permute-start | bytes 1671176 | tf_op jit(solution)/shard_map/ppermute | solution.py:342
  21.4 4.7 %bands.1 = (bf16[8,256,256]{2,1,0:T(8,128)(2,1)}, bf16[16,144,256]{2,1,0:T(8,128)(2,1)}, bf16[16,128,256]{2,1,0:T(8,128)(2,1)}, bf16[8,768,256]{2,1,0:T(8,128)(2,1)}) custom-call(bf16[16,21]{1,0:T(8,128)(2,1)} %row_ref.1, bf16[16,21]{1,0:T(8,128)(2,1)} %col_ref.1), custom_call_target="tpu_custom_call" | custom-call | tf_op jit(solution)/shard_map/bands/pallas_call | solution.py:112
  26.1 0.0 collective-permute-done.2.near_hbm
  26.1 8.9 %collective-permute-done.3.far_hbm = bf16[17,16,1024]{2,1,0:T(8,128)(2,1)S(1)} collective-permute-done((bf16[17,16,1024]{2,1,0:T(8,128)(2,1)S(1)}, bf16[17,16,1024]{2,1,0:T(8,128)(2,1)S(1)}, u32[]{:S(2)}, u32[]{:S(2)}) %collective-permute-start.3) | collective-permute-done | bytes 557088 | tf_op jit(solution)/shard_map/ppermute | solution.py:342
  35.0 0.0 all-to-all-done
  35.0 17.9 %main.1 = (f32[1,256,1024]{2,1,0:T(8,128)}, bf16[1024,256]{1,0:T(8,128)(2,1)}) custom-call(s32[1,1]{1,0:T(1,128)} %bitcast.1.even_ref, bf16[1024,384]{1,0:T(8,128)(2,1)S(1)} %bitcast.14, s32[1,256]{1,0:T(1,128)} %valid_ref.1, bf16[8,256,256]{2,1,0:T(8,128)(2,1)} %get-tuple-element.8.f_hbm, bf16[16,144,256]{2,1,0:T(8,128)(2,1)} %get-tuple-element.9.c_hbm, ...), custom_call_target="tpu_custom_call" | custom-call | tf_op jit(solution)/shard_map/main/pallas_call | solution.py:270
  52.9 18.8 %all_to_all.10.terms_ref = bf16[32,32,256]{2,1,0:T(8,128)(2,1)S(1)} all-to-all(bf16[32,32,256]{2,1,0:T(8,128)(2,1)} %bitcast.15), channel_id=1, replica_groups=mesh['exp'=32,'row'=4] {'exp'}, dimensions={0} | all-to-all | bytes 1048576 | tf_op jit(solution)/shard_map/all_to_all | solution.py:352
  71.7 1.5 %gather.1 = f32[4,32,256]{2,1,0:T(8,128)} custom-call(s32[1,32]{1,0:T(1,128)} %bitcast.21, bf16[32,32,256]{2,1,0:T(8,128)(2,1)S(1)} %all_to_all.10.terms_ref), custom_call_target="tpu_custom_call" | custom-call | tf_op jit(solution)/shard_map/gather/pallas_call | solution.py:311
Async XLA Ops:
  0.6 7.3 %collective-permute-start.1 = (bf16[4,32,256]{2,1,0:T(8,128)(2,1)}, bf16[4,32,256]{2,1,0:T(8,128)(2,1)S(1)}, u32[]{:S(2)}, u32[]{:S(2)}) collective-permute-start(bf16[4,32,256]{2,1,0:T(8,128)(2,1)} %bitcast.17), channel_id=1, source_target_pairs={{1,2},{2,1},{5,6},{6,5},{9,10},{10,9},{13,14},{14,13},{17,18},{18,... | collective-permute-start | bytes 196616 | tf_op jit(solution)/shard_map/ppermute | solution.py:338
  2.6 5.4 %collective-permute-start = (bf16[4,32,256]{2,1,0:T(8,128)(2,1)}, bf16[4,32,256]{2,1,0:T(8,128)(2,1)S(1)}, u32[]{:S(2)}, u32[]{:S(2)}) collective-permute-start(bf16[4,32,256]{2,1,0:T(8,128)(2,1)} %bitcast.18), channel_id=1, source_target_pairs={{0,1},{1,0},{2,3},{3,2},{4,5},{5,4},{6,7},{7,6},{8,9},{9,8},{10,11... | collective-permute-start | bytes 196616 | tf_op jit(solution)/shard_map/ppermute | solution.py:339
  5.6 20.5 %collective-permute-start.2 = (bf16[17,16,1024]{2,1,0:T(8,128)(2,1)S(1)}, bf16[17,16,1024]{2,1,0:T(8,128)(2,1)S(1)}, u32[]{:S(2)}, u32[]{:S(2)}) collective-permute-start(bf16[17,16,1024]{2,1,0:T(8,128)(2,1)S(1)} %maximum_multiply_fusion), channel_id=1, source_target_pairs={{0,1},{1,0},{2,3},{3,2},{4,5},{5,4},{6,7},{7,6},{8,9},{9,8},{10,11... | collective-permute-start | bytes 1671176 | tf_op jit(solution)/shard_map/ppermute | solution.py:343
  9.8 25.2 %all-to-all-start = ((bf16[32,32,384]{2,1,0:T(8,128)(2,1)}), bf16[32,32,384]{2,1,0:T(8,128)(2,1)S(1)}, u32[]{:S(2)}, u32[]{:S(2)}) async-start(bf16[32,32,384]{2,1,0:T(8,128)(2,1)} %pack.1), calls=%async_computation | async-start | bytes 1572864 | tf_op jit(solution)/shard_map/all_to_all | solution.py:346
  18.9 16.1 %collective-permute-start.3 = (bf16[17,16,1024]{2,1,0:T(8,128)(2,1)S(1)}, bf16[17,16,1024]{2,1,0:T(8,128)(2,1)S(1)}, u32[]{:S(2)}, u32[]{:S(2)}) collective-permute-start(bf16[17,16,1024]{2,1,0:T(8,128)(2,1)S(1)} %maximum_multiply_fusion.1), channel_id=1, source_target_pairs={{1,2},{2,1},{5,6},{6,5},{9,10},{10,9},{13,14},{14,13},{17,18},{18,... | collective-permute-start | bytes 1671176 | tf_op jit(solution)/shard_map/ppermute | solution.py:342
where the time goes:
time: 73.7 us; the launch traced here: 73.2 us
  Pallas kernels  26 us (35%)
  blocking collectives  18.8 us (26%)
  starting transfers between devices  14 us (19%)
  waiting for transfers between devices  10.6 us (14%)
  local copies, waits for them, and re-layouts  2.06 us (3%)
  other arithmetic  0.97 us (1%)
    all_to_all x1, blocking collectives, body(): lax.all_to_all(send.reshape(EXPOSURES, OWN, ROWS), 'exp', 0, 0, tiled=True)  18.8 us
    pallas_call x1, Pallas kernels, main(): pl.pallas_call(main_kernel, out_shape=(jax.ShapeDtypeStruct((1, ROWS, COL...  17.9 us
    all_to_all x1, starting transfers between devices, body(): strip = lax.all_to_all(packed, 'exp', 0, 0, tiled=True)  8.97 us
    ppermute x1, waiting for transfers between devices, body(): far_rim = lax.ppermute(far_rim, 'row', across)  8.86 us
    pallas_call x1, Pallas kernels, make_bands(): pl.pallas_call(bands_kernel, out_shape=(jax.ShapeDtypeStruct((PAIRS, 256,...  4.69 us
    ppermute x1, starting transfers between devices, body(): far_rim = lax.ppermute(far_rim, 'row', across)  2.49 us
    ppermute x1, starting transfers between devices, body(): far_sky = lax.ppermute(latent, 'row', across)  1.92 us
    pallas_call x1, Pallas kernels, pack(): pl.pallas_call(pack_kernel, out_shape=jax.ShapeDtypeStruct((EXPOSURES, OW...  1.91 us
  transfers between devices with their start and end apart: 5, of which 2 were waited for; matrix products, arithmetic and copies ran while one was open for 4% of the time, Pallas kernels for 9%

commit v1 on v0

v1 whole, which is shorter than its diff:
```python
import jax
import jax.numpy as jnp
from jax import lax
from jax.experimental import pallas as pl
from jax.experimental.pallas import tpu as pltpu
from jax.sharding import PartitionSpec as P


F32 = jnp.float32
BF16 = jnp.bfloat16
KERNELS = 16
PAIRS = KERNELS // 2
TAPS = 21
HALF = TAPS // 2
CELLS = 4
EXPOSURES = 32
ROWS = 256
COLS = 1024
BLOCKS = COLS // 128
OWN = COLS // EXPOSURES
SKY = 24
RIM = 16
LAT = ROWS + 2 * SKY
EXT = ROWS + 2 * RIM
HOUT = EXT // 2
RBR = ROWS // 2 + 256
LEAD = 32
WR = HOUT + 256
EDGE = 8

VMEM = pl.BlockSpec(memory_space=pltpu.VMEM)
SMEM = pl.BlockSpec(memory_space=pltpu.SMEM)
ANY = pl.BlockSpec(memory_space=pl.ANY)
HBM = pl.BlockSpec(memory_space=pltpu.HBM)


def dot(a, b):
    return lax.dot_general(a, b, (((1,), (0,)), ((), ())), preferred_element_type=F32)


def column_of(valid):
    return jnp.broadcast_to(valid, (128, valid.shape[1])).T


def pack_kernel(even_ref, cell_ref, lat_ref, near_ref, far_ref, out_ref, turned):
    even = even_ref[0, 0] > 0
    fill = jnp.zeros((OWN, 64 - 2 * SKY), F32)
    for c in range(CELLS):
        near, far = near_ref[c].astype(F32), far_ref[c].astype(F32)
        above = jnp.where(even, far[:, ROWS - SKY :], near[:, ROWS - SKY :])
        below = jnp.where(even, near[:, :SKY], far[:, :SKY])
        edges = jnp.concatenate([above, below, fill], axis=1)
        turned[c, 0:OWN, :] = lat_ref[c]
        turned[c, OWN:, :] = jnp.concatenate(
            [edges[EDGE * g : EDGE * g + EDGE] for g in range(OWN // EDGE)], axis=1
        ).astype(BF16)
    for e in range(EXPOSURES):
        out_ref[e] = turned[cell_ref[0, e]]


def pack(even, cell_of, latent, near, far):
    return pl.pallas_call(
        pack_kernel,
        out_shape=jax.ShapeDtypeStruct((EXPOSURES, OWN + EDGE, ROWS), BF16),
        in_specs=[SMEM, SMEM, VMEM, VMEM, VMEM],
        out_specs=VMEM,
        scratch_shapes=[pltpu.VMEM((CELLS, OWN + EDGE, ROWS), BF16)],
        name="pack",
    )(even, cell_of, latent, near, far)


def base_rows(taps, place):
    lane = lax.broadcasted_iota(jnp.int32, (KERNELS, 256), 1)
    out = jnp.zeros((KERNELS, 256), F32)
    for t in range(TAPS):
        out = jnp.where(lane == place(t) % 256, taps[:, t : t + 1], out)
    return out


def skewed(row, count):
    return pltpu.roll(jnp.broadcast_to(row, (count, 256)), 0, 1, stride=1, stride_axis=0)


def bands_kernel(row_ref, col_ref, f_ref, c_hbm, a_hbm, b_hbm, c_ref, a_ref, b_ref, sem):
    c_out = pltpu.make_async_copy(c_ref, c_hbm, sem.at[PAIRS + 1])
    a_out = pltpu.make_async_copy(a_ref, a_hbm, sem.at[PAIRS])
    b_out = [pltpu.make_async_copy(b_ref.at[i], b_hbm.at[i], sem.at[i]) for i in range(PAIRS)]
    rows = row_ref[...].astype(F32)
    cols = col_ref[...].astype(F32)
    f_base = base_rows(rows, lambda t: HALF - t)
    b_base = base_rows(rows, lambda t: t - HALF)
    c_base = base_rows(cols, lambda t: t + SKY - HALF)
    a_base = base_rows(cols, lambda t: LEAD - RIM + HALF - t)
    at = lax.broadcasted_iota(jnp.int32, (256, 256), 0)
    out = lax.broadcasted_iota(jnp.int32, (256, 256), 1)
    near = jnp.abs(at - out) < 128
    for k in range(KERNELS):
        i, q = k // 2, k % 2
        f_ref[i, :, 128 * q : 128 * q + 128] = skewed(f_base[k : k + 1], 256)[:, :128].astype(BF16)
        b = skewed(b_base[k : k + 1], 256)
        b_ref[i, 256 * q : 256 * q + 256, :] = jnp.where(near, b, 0.0).astype(BF16)
        far = jnp.where(near, 0.0, b).astype(BF16)
        b_ref[i, 512 + 128 * q : 576 + 128 * q, :] = far[:64]
        b_ref[i, 576 + 128 * q : 640 + 128 * q, :] = far[192:]
        c_ref[k] = skewed(c_base[k : k + 1], 128).astype(BF16)
        a_ref[k] = skewed(a_base[k : k + 1], HOUT).astype(BF16)
        if q == 1:
            b_out[i].start()
    c_out.start()
    a_out.start()
    for copy in (*b_out, c_out, a_out):
        copy.wait()


def make_bands(row_taps, column_taps):
    return pl.pallas_call(
        bands_kernel,
        out_shape=(
            jax.ShapeDtypeStruct((PAIRS, 256, 256), BF16),
            jax.ShapeDtypeStruct((KERNELS, 128, 256), BF16),
            jax.ShapeDtypeStruct((KERNELS, HOUT, 256), BF16),
            jax.ShapeDtypeStruct((PAIRS, 768, 256), BF16),
        ),
        in_specs=[VMEM, VMEM],
        out_specs=(VMEM, HBM, HBM, HBM),
        scratch_shapes=[
            pltpu.VMEM((KERNELS, 128, 256), BF16),
            pltpu.VMEM((KERNELS, HOUT, 256), BF16),
            pltpu.VMEM((PAIRS, 768, 256), BF16),
            pltpu.SemaphoreType.DMA((PAIRS + 2,)),
        ],
        compiler_params=pltpu.CompilerParams(vmem_limit_bytes=56 << 20),
        name="bands",
    )(row_taps, column_taps)


def main_kernel(
    even_ref, strip_ref, valid_ref, f_hbm, c_hbm, a_hbm, b_hbm, coef_hbm, obs_hbm,
    res_hbm, term_ref, near_ref, far_ref,
    f_ref, c_ref, a_ref, b_ref, sky, windows, coef, obs, rb, rb2, pred, w, w2, cb, cb2, acc, sem, band_sem,
):
    def coef_in(k):
        return pltpu.make_async_copy(coef_hbm.at[0, k], coef.at[k], sem.at[k])

    pairs = ((f_hbm, f_ref), (c_hbm, c_ref), (obs_hbm.at[0], obs), (a_hbm, a_ref), (b_hbm, b_ref))
    first = [pltpu.make_async_copy(s, d, band_sem.at[n]) for n, (s, d) in enumerate(pairs)]
    for copy in first[:3]:
        copy.start()
    for k in range(KERNELS):
        coef_in(k).start()
    for copy in first[3:]:
        copy.start()

    for r in (rb, rb2):
        r[:, :, LAT:, :] = jnp.zeros((2, BLOCKS, RBR - LAT, 128), BF16)
    for r in (w, w2):
        r[:, :, 0:LEAD, :] = jnp.zeros((2, BLOCKS, LEAD, 128), BF16)
        r[:, :, LEAD + ROWS :, :] = jnp.zeros((2, BLOCKS, WR - LEAD - ROWS, 128), BF16)
    acc[...] = jnp.zeros_like(acc)
    low = lax.broadcasted_iota(jnp.int32, (LAT, 128), 1) < 64
    for j in range(BLOCKS):
        own, edges = [], []
        for e in range(4 * j, 4 * j + 4):
            own.append(strip_ref[e, 0:OWN, :].astype(F32))
            edge = strip_ref[e, OWN:, :].astype(F32)
            edges += [edge[:, 64 * g : 64 * g + 64] for g in range(OWN // EDGE)]
        edges = jnp.concatenate(edges, axis=0).T
        sky[j, 0:SKY, :] = edges[0:SKY]
        sky[j, SKY : SKY + ROWS, :] = jnp.concatenate(own, axis=0).T
        sky[j, SKY + ROWS :, :] = edges[SKY : 2 * SKY]
    zero = jnp.zeros((LAT, 128), F32)
    for j in range(BLOCKS):
        after = sky[j + 1] if j + 1 < BLOCKS else zero
        before = sky[j - 1] if j > 0 else zero
        windows[j, :, 0:128] = sky[j].astype(BF16)
        windows[j, :, 128:256] = jnp.where(low, after, before).astype(BF16)
    for copy in first[:3]:
        copy.wait()
    pred[...] = -obs[...].astype(F32)

    def blur(i, rb):
        f = f_ref[i]
        for j in range(BLOCKS):
            both = dot(windows[j], f)
            rb[0, j, 0:LAT, :] = both[:, :128].astype(BF16)
            rb[1, j, 0:LAT, :] = both[:, 128:].astype(BF16)

    def predict(i, rb):
        for q in range(2):
            k = 2 * i + q
            c = c_ref[k]
            for h in range(2):
                out = slice(128 * h, 128 * h + 128)
                for x in range(0, BLOCKS, 2):
                    at = slice(128 * h, 128 * h + 256)
                    v = dot(c, jnp.concatenate([rb[q, x, at, :], rb[q, x + 1, at, :]], axis=1))
                    cols = slice(128 * x, 128 * x + 256)
                    pred[out, cols] += coef[k, out, cols].astype(F32) * v

    def forward(n, carry):
        for m in range(4):
            coef_in(4 * n + m).wait()
        blur(2 * n, rb)
        blur(2 * n + 1, rb2)
        predict(2 * n, rb)
        predict(2 * n + 1, rb2)
        return carry

    lax.fori_loop(0, PAIRS // 2, forward, 0)

    mask = column_of(valid_ref[...].astype(F32))
    for j in range(BLOCKS):
        pred[:, 128 * j : 128 * j + 128] *= mask
    res_out = pltpu.make_async_copy(pred, res_hbm.at[0], band_sem.at[0])
    res_out.start()

    low_y = lax.broadcasted_iota(jnp.int32, (EXT, 128), 1) < 64
    none = jnp.zeros((EXT, 128), BF16)

    def weigh(i, w):
        for q in range(2):
            for x in range(BLOCKS):
                cols = slice(128 * x, 128 * x + 128)
                w[q, x, LEAD : LEAD + ROWS, :] = (coef[2 * i + q, :, cols].astype(F32) * pred[:, cols]).astype(BF16)

    def back(i, w, cb):
        for q in range(2):
            a = a_ref[2 * i + q]
            for h in range(2):
                out = slice(HOUT * h, HOUT * h + HOUT)
                at = slice(HOUT * h, HOUT * h + 256)
                for x in range(0, BLOCKS, 2):
                    both = dot(a, jnp.concatenate([w[q, x, at, :], w[q, x + 1, at, :]], axis=1))
                    cb[q, x, out, :] = both[:, :128].astype(BF16)
                    cb[q, x + 1, out, :] = both[:, 128:].astype(BF16)
        b = b_ref[i]
        for x in range(0, BLOCKS, 2):
            parts = [cb[0, x], cb[0, x + 1], cb[1, x], cb[1, x + 1]]
            for q in range(2):
                after = cb[q, x + 2] if x + 2 < BLOCKS else none
                before = cb[q, x - 1] if x > 0 else none
                parts.append(jnp.where(low_y, after, before))
            acc[x // 2] += dot(jnp.concatenate(parts, axis=1), b)

    weigh(0, w)
    for copy in first[3:]:
        copy.wait()

    def adjoint(n, carry):
        weigh(2 * n + 1, w2)
        back(2 * n, w, cb)
        weigh(jnp.minimum(2 * n + 2, PAIRS - 1), w)
        back(2 * n + 1, w2, cb2)
        return carry

    lax.fori_loop(0, PAIRS // 2, adjoint, 0)
    even = even_ref[0, 0] > 0
    for x in range(BLOCKS // 2):
        head, tail = acc[x, 0:RIM, :], acc[x, RIM + ROWS :, :]
        near_ref[x] = jnp.where(even, tail, head)
        far_ref[x] = jnp.where(even, head, tail)
        term_ref[x] = acc[x, RIM : RIM + ROWS, :]
    res_out.wait()


def main(even, strip, valid, bands, coefficients, observed):
    rim = jax.ShapeDtypeStruct((BLOCKS // 2, RIM, 256), F32)
    return pl.pallas_call(
        main_kernel,
        out_shape=(
            jax.ShapeDtypeStruct((1, ROWS, COLS), F32),
            jax.ShapeDtypeStruct((BLOCKS // 2, ROWS, 256), F32),
            rim,
            rim,
        ),
        in_specs=[SMEM] + [VMEM] * 2 + [HBM] * 6,
        out_specs=(HBM, VMEM, VMEM, VMEM),
        scratch_shapes=[
            pltpu.VMEM((PAIRS, 256, 256), BF16),
            pltpu.VMEM((KERNELS, 128, 256), BF16),
            pltpu.VMEM((KERNELS, HOUT, 256), BF16),
            pltpu.VMEM((PAIRS, 768, 256), BF16),
            pltpu.VMEM((BLOCKS, LAT, 128), F32),
            pltpu.VMEM((BLOCKS, LAT, 256), BF16),
            pltpu.VMEM((KERNELS, ROWS, COLS), BF16),
            pltpu.VMEM((ROWS, COLS), BF16),
            pltpu.VMEM((2, BLOCKS, RBR, 128), BF16),
            pltpu.VMEM((2, BLOCKS, RBR, 128), BF16),
            pltpu.VMEM((ROWS, COLS), F32),
            pltpu.VMEM((2, BLOCKS, WR, 128), BF16),
            pltpu.VMEM((2, BLOCKS, WR, 128), BF16),
            pltpu.VMEM((2, BLOCKS, EXT, 128), BF16),
            pltpu.VMEM((2, BLOCKS, EXT, 128), BF16),
            pltpu.VMEM((BLOCKS // 2, EXT, 256), F32),
            pltpu.SemaphoreType.DMA((KERNELS,)),
            pltpu.SemaphoreType.DMA((5,)),
        ],
        compiler_params=pltpu.CompilerParams(vmem_limit_bytes=56 << 20),
        name="main",
    )(even, strip, valid, *bands, coefficients, observed)


def finish_kernel(even_ref, term_ref, near_ref, far_ref, send_ref):
    even = even_ref[0, 0] > 0
    for x in range(BLOCKS // 2):
        near, far = near_ref[x], far_ref[x]
        top = term_ref[x, 0:RIM, :] + jnp.where(even, far, near)
        bottom = term_ref[x, ROWS - RIM :, :] + jnp.where(even, near, far)
        whole = jnp.concatenate([top, term_ref[x, RIM : ROWS - RIM, :], bottom], axis=0)
        send_ref[256 * x : 256 * x + 256, :] = whole.T.astype(BF16)


def finish(even, term, near, far):
    return pl.pallas_call(
        finish_kernel,
        out_shape=jax.ShapeDtypeStruct((COLS, ROWS), BF16),
        in_specs=[SMEM, VMEM, VMEM, VMEM],
        out_specs=VMEM,
        name="finish",
    )(even, term, near, far)


def gather_kernel(cell_ref, terms_ref, out_ref):
    out_ref[...] = jnp.zeros_like(out_ref)
    for e in range(EXPOSURES):
        out_ref[cell_ref[0, e]] += terms_ref[e].astype(F32)


def gather(cell_of, terms):
    return pl.pallas_call(
        gather_kernel,
        out_shape=jax.ShapeDtypeStruct((CELLS, OWN, ROWS), F32),
        in_specs=[SMEM, VMEM],
        out_specs=VMEM,
        name="gather",
    )(cell_of, terms)


def keep(*arrays):
    return [pltpu.with_memory_space_constraint(a, pltpu.VMEM) for a in arrays]


def body(latent, row_taps, column_taps, coefficients, observed, cell_of, valid_rows):
    count = lax.axis_size("row")
    even = 1 - lax.rem(lax.axis_index("row"), 2)
    chip = [(i, i ^ 1) for i in range(count)]
    across = [(i, i + 1) for i in range(1, count - 1, 2)] + [(i + 1, i) for i in range(1, count - 1, 2)]
    cell_of = cell_of.reshape(1, EXPOSURES)
    latent = jnp.swapaxes(latent, 1, 2)

    far_sky = lax.ppermute(latent, "row", across)
    near_sky = lax.ppermute(latent, "row", chip)
    even = even.reshape(1, 1)
    packed = pack(even, cell_of, latent, *keep(near_sky, far_sky))
    strip = lax.all_to_all(packed, "exp", 0, 0, tiled=True)
    bands = make_bands(row_taps, column_taps)
    residual, *terms = main(even, *keep(strip), valid_rows, bands, coefficients, observed)
    term, near, far = keep(*terms)
    far = lax.ppermute(far, "row", across)
    near = lax.ppermute(near, "row", chip)
    send = finish(even, *keep(term, near, far)).reshape(EXPOSURES, OWN, ROWS)
    terms = lax.all_to_all(send, "exp", 0, 0, tiled=True)
    return jnp.swapaxes(gather(cell_of, *keep(terms)), 1, 2), residual


def solution(mesh):
    placed = (
        P(None, "row", "exp"),
        P(),
        P(),
        P("exp", None, "row", None),
        P("exp", "row", None),
        P(),
        P("exp", "row"),
    )
    return jax.shard_map(
        body,
        mesh=mesh,
        in_specs=placed,
        out_specs=(P(None, "row", "exp"), P("exp", "row", None)),
        check_vma=False,
    )
```

time: 73.7 us -> 76.9 us (1.043)
  the two profiles are of different devices: /device:TPU:4 before, /device:TPU:1 now
where the time goes in v1:
time: 76.9 us; the launch traced here: 76.4 us
  Pallas kernels  28.7 us (37%)
  starting transfers between devices  19.1 us (25%)
  blocking collectives  14.2 us (18%)
  waiting for transfers between devices  12.6 us (16%)
  local copies, waits for them, and re-layouts  1.22 us (2%)
    pallas_call x1, Pallas kernels, main(): pl.pallas_call(main_kernel, out_shape=(jax.ShapeDtypeStruct((1, ROWS, COL...  19.5 us
    all_to_all x1, blocking collectives, body(): terms = lax.all_to_all(send, 'exp', 0, 0, tiled=True)  14.2 us
    all_to_all x1, starting transfers between devices, body(): strip = lax.all_to_all(packed, 'exp', 0, 0, tiled=True)  8.92 us
    all_to_all x1, waiting for transfers between devices, body(): strip = lax.all_to_all(packed, 'exp', 0, 0, tiled=True)  7.12 us
    ppermute x1, starting transfers between devices, body(): far_sky = lax.ppermute(latent, 'row', across)  6.03 us
    pallas_call x1, Pallas kernels, make_bands(): pl.pallas_call(bands_kernel, out_shape=(jax.ShapeDtypeStruct((PAIRS, 256,...  4.72 us
    ppermute x1, starting transfers between devices, body(): far = lax.ppermute(far, 'row', across)  3.82 us
    ppermute x1, waiting for transfers between devices, body(): far = lax.ppermute(far, 'row', across)  3.45 us
  transfers between devices with their start and end apart: 5, of which 3 were waited for; matrix products, arithmetic and copies ran while one was open for 0% of the time, Pallas kernels for 6%

profile of v1, /device:TPU:1, one launch (start us, length us, event | category | flops | bytes accessed | tf_op | source)
XLA Modules:
  0.0 76.4 jit_solution(9925627325426032151)
XLA Ops:
  0.6 6.0 %collective-permute-start.1 = (bf16[4,32,256]{2,1,0:T(8,128)(2,1)}, bf16[4,32,256]{2,1,0:T(8,128)(2,1)S(1)}, u32[]{:S(2)}, u32[]{:S(2)}) collective-permute-start(bf16[4,32,256]{2,1,0:T(8,128)(2,1)} %bitcast.7), channel_id=1, source_target_pairs={{1,2},{2,1},{5,6},{6,5},{9,10},{10,9},{13,14},{14,13},{17,18},{18,... | collective-permute-start | bytes 196616 | tf_op jit(solution)/shard_map/ppermute | solution.py:351
  6.7 0.1 collective-permute-start
  6.8 2.0 %collective-permute-done.1.far_ref = bf16[4,32,256]{2,1,0:T(8,128)(2,1)S(1)} collective-permute-done((bf16[4,32,256]{2,1,0:T(8,128)(2,1)}, bf16[4,32,256]{2,1,0:T(8,128)(2,1)S(1)}, u32[]{:S(2)}, u32[]{:S(2)}) %collective-permute-start.1) | collective-permute-done | bytes 65568 | tf_op jit(solution)/shard_map/ppermute | solution.py:351
  8.8 0.0 collective-permute-done.near_ref
  8.8 1.9 %pack.1 = bf16[32,40,256]{2,1,0:T(8,128)(2,1)} custom-call(s32[1,1]{1,0:T(1,128)} %bitcast.1.even_ref, s32[1,32]{1,0:T(1,128)} %bitcast.10, bf16[4,32,256]{2,1,0:T(8,128)(2,1)} %bitcast.9, bf16[4,32,256]{2,1,0:T(8,128)(2,1)S(1)} %collective-permute-done.near_ref, bf16[4,32,256]{2,1,0:T(8,128)(2,1)S(1)} %collective-permute-done.1.far_ref), custom_call_target="tpu_custom_call" | custom-call | tf_op jit(solution)/shard_map/pack/pallas_call | solution.py:62
  10.7 8.9 %all-to-all-start = ((bf16[32,40,256]{2,1,0:T(8,128)(2,1)}), bf16[32,40,256]{2,1,0:T(8,128)(2,1)S(1)}, u32[]{:S(2)}, u32[]{:S(2)}) async-start(bf16[32,40,256]{2,1,0:T(8,128)(2,1)} %pack.1), calls=%async_computation | async-start | bytes 1310720 | tf_op jit(solution)/shard_map/all_to_all | solution.py:355
  19.6 4.7 %bands.1 = (bf16[8,256,256]{2,1,0:T(8,128)(2,1)}, bf16[16,128,256]{2,1,0:T(8,128)(2,1)}, bf16[16,144,256]{2,1,0:T(8,128)(2,1)}, bf16[8,768,256]{2,1,0:T(8,128)(2,1)}) custom-call(bf16[16,21]{1,0:T(8,128)(2,1)} %row_ref.1, bf16[16,21]{1,0:T(8,128)(2,1)} %col_ref.1), custom_call_target="tpu_custom_call" | custom-call | tf_op jit(solution)/shard_map/bands/pallas_call | solution.py:116
  24.3 7.1 %all-to-all-done.strip_ref = bf16[32,40,256]{2,1,0:T(8,128)(2,1)S(1)} async-done(((bf16[32,40,256]{2,1,0:T(8,128)(2,1)}), bf16[32,40,256]{2,1,0:T(8,128)(2,1)S(1)}, u32[]{:S(2)}, u32[]{:S(2)}) %all-to-all-start) | async-done | bytes 655392 | tf_op jit(solution)/shard_map/all_to_all | solution.py:355
  31.5 19.5 %main.1 = (f32[1,256,1024]{2,1,0:T(8,128)}, f32[4,256,256]{2,1,0:T(8,128)}, f32[4,16,256]{2,1,0:T(8,128)}, f32[4,16,256]{2,1,0:T(8,128)}) custom-call(s32[1,1]{1,0:T(1,128)} %bitcast.1.even_ref, bf16[32,40,256]{2,1,0:T(8,128)(2,1)S(1)} %all-to-all-done.strip_ref, s32[1,256]{1,0:T(1,128)} %valid_ref.1, bf16[8,256,256]{2,1,0:T(8,128)(2,1)} %get-tuple-element.10.f_hbm, ...), custom_call_target="tpu_custom_call" | custom-call | tf_op jit(solution)/shard_map/main/pallas_call | solution.py:268
  51.0 0.2 collective-permute-start.2
  51.2 3.8 %collective-permute-start.3 = (f32[4,16,256]{2,1,0:T(8,128)}, f32[4,16,256]{2,1,0:T(8,128)S(1)}, u32[]{:S(2)}, u32[]{:S(2)}) collective-permute-start(f32[4,16,256]{2,1,0:T(8,128)} %get-tuple-element.16), channel_id=1, source_target_pairs={{1,2},{2,1},{5,6},{6,5},{9,10},{10,9},{13,14},{14,13},{17,18},{18,... | collective-permute-start | bytes 196616 | tf_op jit(solution)/shard_map/ppermute | solution.py:359
  55.1 0.0 collective-permute-done.2.near_ref
  55.1 3.4 %collective-permute-done.3.far_ref = f32[4,16,256]{2,1,0:T(8,128)S(1)} collective-permute-done((f32[4,16,256]{2,1,0:T(8,128)}, f32[4,16,256]{2,1,0:T(8,128)S(1)}, u32[]{:S(2)}, u32[]{:S(2)}) %collective-permute-start.3) | collective-permute-done | bytes 65568 | tf_op jit(solution)/shard_map/ppermute | solution.py:359
  58.5 0.0 copy-start
  58.5 1.2 %copy-done = f32[4,256,256]{2,1,0:T(8,128)S(1)} copy-done((f32[4,256,256]{2,1,0:T(8,128)S(1)}, f32[4,256,256]{2,1,0:T(8,128)}, u32[]{:S(2)}) %copy-start) | copy-done | bytes 1048600
  59.7 1.0 %finish.1 = bf16[1024,256]{1,0:T(8,128)(2,1)} custom-call(s32[1,1]{1,0:T(1,128)} %bitcast.1.even_ref, f32[4,256,256]{2,1,0:T(8,128)S(1)} %copy-done, f32[4,16,256]{2,1,0:T(8,128)S(1)} %collective-permute-done.2.near_ref, f32[4,16,256]{2,1,0:T(8,128)S(1)} %collective-permute-done.3.far_ref), custom_call_target="tpu_custom_call" | custom-call | tf_op jit(solution)/shard_map/finish/pallas_call | solution.py:314
  60.8 14.2 %all_to_all.10.terms_ref = bf16[32,32,256]{2,1,0:T(8,128)(2,1)S(1)} all-to-all(bf16[32,32,256]{2,1,0:T(8,128)(2,1)} %bitcast.5), channel_id=1, replica_groups=mesh['exp'=32,'row'=4] {'exp'}, dimensions={0} | all-to-all | bytes 1048576 | tf_op jit(solution)/shard_map/all_to_all | solution.py:362
  74.9 1.5 %gather.1 = f32[4,32,256]{2,1,0:T(8,128)} custom-call(s32[1,32]{1,0:T(1,128)} %bitcast.11, bf16[32,32,256]{2,1,0:T(8,128)(2,1)S(1)} %all_to_all.10.terms_ref), custom_call_target="tpu_custom_call" | custom-call | tf_op jit(solution)/shard_map/gather/pallas_call | solution.py:330
Async XLA Ops:
  0.6 8.2 %collective-permute-start.1 = (bf16[4,32,256]{2,1,0:T(8,128)(2,1)}, bf16[4,32,256]{2,1,0:T(8,128)(2,1)S(1)}, u32[]{:S(2)}, u32[]{:S(2)}) collective-permute-start(bf16[4,32,256]{2,1,0:T(8,128)(2,1)} %bitcast.7), channel_id=1, source_target_pairs={{1,2},{2,1},{5,6},{6,5},{9,10},{10,9},{13,14},{14,13},{17,18},{18,... | collective-permute-start | bytes 196616 | tf_op jit(solution)/shard_map/ppermute | solution.py:351
  6.7 2.1 %collective-permute-start = (bf16[4,32,256]{2,1,0:T(8,128)(2,1)}, bf16[4,32,256]{2,1,0:T(8,128)(2,1)S(1)}, u32[]{:S(2)}, u32[]{:S(2)}) collective-permute-start(bf16[4,32,256]{2,1,0:T(8,128)(2,1)} %bitcast.8), channel_id=1, source_target_pairs={{0,1},{1,0},{2,3},{3,2},{4,5},{5,4},{6,7},{7,6},{8,9},{9,8},{10,11... | collective-permute-start | bytes 196616 | tf_op jit(solution)/shard_map/ppermute | solution.py:352
  10.7 20.8 %all-to-all-start = ((bf16[32,40,256]{2,1,0:T(8,128)(2,1)}), bf16[32,40,256]{2,1,0:T(8,128)(2,1)S(1)}, u32[]{:S(2)}, u32[]{:S(2)}) async-start(bf16[32,40,256]{2,1,0:T(8,128)(2,1)} %pack.1), calls=%async_computation | async-start | bytes 1310720 | tf_op jit(solution)/shard_map/all_to_all | solution.py:355
  51.0 4.1 %collective-permute-start.2 = (f32[4,16,256]{2,1,0:T(8,128)}, f32[4,16,256]{2,1,0:T(8,128)S(1)}, u32[]{:S(2)}, u32[]{:S(2)}) collective-permute-start(f32[4,16,256]{2,1,0:T(8,128)} %get-tuple-element.15), channel_id=1, source_target_pairs={{0,1},{1,0},{2,3},{3,2},{4,5},{5,4},{6,7},{7,6},{8,9},{9,8},{10,11... | collective-permute-start | bytes 196616 | tf_op jit(solution)/shard_map/ppermute | solution.py:360
  51.2 7.3 %collective-permute-start.3 = (f32[4,16,256]{2,1,0:T(8,128)}, f32[4,16,256]{2,1,0:T(8,128)S(1)}, u32[]{:S(2)}, u32[]{:S(2)}) collective-permute-start(f32[4,16,256]{2,1,0:T(8,128)} %get-tuple-element.16), channel_id=1, source_target_pairs={{1,2},{2,1},{5,6},{6,5},{9,10},{10,9},{13,14},{14,13},{17,18},{18,... | collective-permute-start | bytes 196616 | tf_op jit(solution)/shard_map/ppermute | solution.py:359
  58.5 1.2 %copy-start = (f32[4,256,256]{2,1,0:T(8,128)S(1)}, f32[4,256,256]{2,1,0:T(8,128)}, u32[]{:S(2)}) copy-start(f32[4,256,256]{2,1,0:T(8,128)} %get-tuple-element.14.term_ref) | copy-start | bytes 3145732

commit v2 on v0

--- a/solution.py
+++ b/solution.py
@@ -21,7 +21,7 @@
 SKY = 24
 RIM = 16
 LAT = ROWS + 2 * SKY
-LATP = 384
+EDGE = 8
 EXT = ROWS + 2 * RIM
 HOUT = EXT // 2
 TOP = 8
@@ -44,12 +44,16 @@
 
 def pack_kernel(even_ref, cell_ref, lat_ref, near_ref, far_ref, out_ref, turned):
     even = even_ref[0, 0] > 0
-    fill = jnp.zeros((OWN, LATP - LAT), F32)
+    fill = jnp.zeros((OWN, 64 - 2 * SKY), F32)
     for c in range(CELLS):
         near, far = near_ref[c].astype(F32), far_ref[c].astype(F32)
         above = jnp.where(even, far[:, ROWS - SKY :], near[:, ROWS - SKY :])
         below = jnp.where(even, near[:, :SKY], far[:, :SKY])
-        turned[c] = jnp.concatenate([above, lat_ref[c].astype(F32), below, fill], axis=1).astype(BF16)
+        edges = jnp.concatenate([above, below, fill], axis=1)
+        turned[c, 0:OWN, :] = lat_ref[c]
+        turned[c, OWN:, :] = jnp.concatenate(
+            [edges[EDGE * g : EDGE * g + EDGE] for g in range(OWN // EDGE)], axis=1
+        ).astype(BF16)
     for e in range(EXPOSURES):
         out_ref[e] = turned[cell_ref[0, e]]
 
@@ -57,10 +61,10 @@
 def pack(even, cell_of, latent, near, far):
     return pl.pallas_call(
         pack_kernel,
-        out_shape=jax.ShapeDtypeStruct((EXPOSURES, OWN, LATP), BF16),
+        out_shape=jax.ShapeDtypeStruct((EXPOSURES, OWN + EDGE, ROWS), BF16),
         in_specs=[SMEM, SMEM, VMEM, VMEM, VMEM],
         out_specs=VMEM,
-        scratch_shapes=[pltpu.VMEM((CELLS, OWN, LATP), BF16)],
+        scratch_shapes=[pltpu.VMEM((CELLS, OWN + EDGE, ROWS), BF16)],
         name="pack",
     )(even, cell_of, latent, near, far)
 
@@ -171,7 +175,15 @@
     acc[...] = jnp.zeros_like(acc)
     low = lax.broadcasted_iota(jnp.int32, (LAT, 128), 1) < 64
     for j in range(BLOCKS):
-        sky[j] = strip_ref[128 * j : 128 * j + 128, :].astype(F32).T[:LAT]
+        own, edges = [], []
+        for e in range(4 * j, 4 * j + 4):
+            own.append(strip_ref[e, 0:OWN, :].astype(F32))
+            edge = strip_ref[e, OWN:, :].astype(F32)
+            edges += [edge[:, 64 * g : 64 * g + 64] for g in range(OWN // EDGE)]
+        edges = jnp.concatenate(edges, axis=0).T
+        sky[j, 0:SKY, :] = edges[0:SKY]
+        sky[j, SKY : SKY + ROWS, :] = jnp.concatenate(own, axis=0).T
+        sky[j, SKY + ROWS :, :] = edges[SKY : 2 * SKY]
     zero = jnp.zeros((LAT, 128), F32)
     for j in range(BLOCKS):
         after = sky[j + 1] if j + 1 < BLOCKS else zero
@@ -339,13 +351,12 @@
     near_sky = lax.ppermute(latent, "row", chip)
     far_rim = rim((1 - even) * (ROWS - RIM))
     near_rim = rim(even * (ROWS - RIM))
-    far_rim = lax.ppermute(far_rim, "row", across)
-    near_rim = lax.ppermute(near_rim, "row", chip)
     even = even.reshape(1, 1)
     packed = pack(even, cell_of, latent, *keep(near_sky, far_sky))
     strip = lax.all_to_all(packed, "exp", 0, 0, tiled=True)
+    far_rim = lax.ppermute(far_rim, "row", across)
+    near_rim = lax.ppermute(near_rim, "row", chip)
     f, c, a, b = make_bands(row_taps, column_taps)
-    strip = strip.reshape(COLS, LATP)
     residual, send = main(
         even, *keep(strip), valid_rows, (f, c, a, b), coefficients, observed, *keep(near_rim, far_rim)
     )

time: 73.7 us -> 72.3 us (0.981)
  waiting for transfers between devices: 10.6 us -> 9.24 us
    ppermute x1, waiting for transfers between devices: 8.86 us -> 7.46 us  [body(): far_rim = lax.ppermute(far_rim, 'row', across)]
where the time goes in v2:
time: 72.3 us; the launch traced here: 71.8 us
  Pallas kernels  26 us (36%)
  blocking collectives  18.8 us (26%)
  starting transfers between devices  14 us (19%)
  waiting for transfers between devices  9.24 us (13%)
  local copies, waits for them, and re-layouts  2.06 us (3%)
  other arithmetic  0.97 us (1%)
    all_to_all x1, blocking collectives, body(): lax.all_to_all(send.reshape(EXPOSURES, OWN, ROWS), 'exp', 0, 0, tiled=True)  18.8 us
    pallas_call x1, Pallas kernels, main(): pl.pallas_call(main_kernel, out_shape=(jax.ShapeDtypeStruct((1, ROWS, COL...  17.9 us
    all_to_all x1, starting transfers between devices, body(): strip = lax.all_to_all(packed, 'exp', 0, 0, tiled=True)  8.97 us
    ppermute x1, waiting for transfers between devices, body(): far_rim = lax.ppermute(far_rim, 'row', across)  7.46 us
    pallas_call x1, Pallas kernels, make_bands(): pl.pallas_call(bands_kernel, out_shape=(jax.ShapeDtypeStruct((PAIRS, 256,...  4.69 us
    ppermute x1, starting transfers between devices, body(): far_rim = lax.ppermute(far_rim, 'row', across)  2.49 us
    ppermute x1, starting transfers between devices, body(): far_sky = lax.ppermute(latent, 'row', across)  1.92 us
    pallas_call x1, Pallas kernels, pack(): pl.pallas_call(pack_kernel, out_shape=jax.ShapeDtypeStruct((EXPOSURES, OW...  1.88 us
  transfers between devices with their start and end apart: 5, of which 2 were waited for; matrix products, arithmetic and copies ran while one was open for 4% of the time, Pallas kernels for 9%

profile of v2, /device:TPU:4, one launch (start us, length us, event | category | flops | bytes accessed | tf_op | source)
XLA Modules:
  0.0 71.8 jit_solution(7188760260069349537)
XLA Ops:
  0.6 1.9 %collective-permute-start.1 = (bf16[4,32,256]{2,1,0:T(8,128)(2,1)}, bf16[4,32,256]{2,1,0:T(8,128)(2,1)S(1)}, u32[]{:S(2)}, u32[]{:S(2)}) collective-permute-start(bf16[4,32,256]{2,1,0:T(8,128)(2,1)} %bitcast.15), channel_id=1, source_target_pairs={{1,2},{2,1},{5,6},{6,5},{9,10},{10,9},{13,14},{14,13},{17,18},{18,... | collective-permute-start | bytes 196616 | tf_op jit(solution)/shard_map/ppermute | solution.py:350
  2.6 0.1 collective-permute-start
  2.7 0.8 %fusion.3 = (bf16[16]{0:T(256)(128)(2,1)S(1)}, bf16[16]{0:T(256)(128)(2,1)S(1)}) fusion(s32[1,256]{1,0:T(1,128)} %valid_ref.1, s32[]{:T(128)S(6)} %select_n.5, s32[]{:T(128)S(6)} %select_n.4), kind=kLoop, calls=%fused_computation.11 | loop fusion | flops 32 | bytes 200 | tf_op jit(solution)/shard_map/convert_element_type | solution.py:347
  3.4 0.8 %constant_dynamic-slice_fusion.1 = (bf16[1,16,1024]{2,1,0:T(8,128)(2,1)S(1)}, bf16[1,16,1024]{2,1,0:T(8,128)(2,1)S(1)}) fusion(bf16[1,256,1024]{2,1,0:T(8,128)(2,1)} %obs_hbm.1, s32[]{:T(128)S(6)} %select_n.5, s32[]{:T(128)S(6)} %select_n.4), kind=kLoop, calls=%fused_computation.5 | loop fusion | bytes 131080 | tf_op jit(solution)/shard_map/dynamic_slice | solution.py:346
  4.2 1.3 %dynamic-slice_bitcast_fusion = (bf16[16,16,1024]{2,1,0:T(8,128)(2,1)S(1)}, bf16[16,16,1024]{2,1,0:T(8,128)(2,1)S(1)}) fusion(bf16[1,16,256,1024]{3,2,1,0:T(8,128)(2,1)} %coef_hbm.1, s32[]{:T(128)S(6)} %select_n.5, s32[]{:T(128)S(6)} %select_n.4), kind=kLoop, calls=%fused_computation.2 | loop fusion | bytes 2097160 | tf_op jit(solution)/shard_map/dynamic_slice | solution.py:345
  5.5 0.1 maximum_multiply_fusion
  5.6 0.6 collective-permute-start.2
  6.2 1.8 %collective-permute-done.1.far_ref = bf16[4,32,256]{2,1,0:T(8,128)(2,1)S(1)} collective-permute-done((bf16[4,32,256]{2,1,0:T(8,128)(2,1)}, bf16[4,32,256]{2,1,0:T(8,128)(2,1)S(1)}, u32[]{:S(2)}, u32[]{:S(2)}) %collective-permute-start.1) | collective-permute-done | bytes 65568 | tf_op jit(solution)/shard_map/ppermute | solution.py:350
  7.9 0.0 collective-permute-done.near_ref
  7.9 1.9 %pack.1 = bf16[32,40,256]{2,1,0:T(8,128)(2,1)} custom-call(s32[1,1]{1,0:T(1,128)} %bitcast.1.even_ref, s32[1,32]{1,0:T(1,128)} %bitcast.18, bf16[4,32,256]{2,1,0:T(8,128)(2,1)} %bitcast.17, bf16[4,32,256]{2,1,0:T(8,128)(2,1)S(1)} %collective-permute-done.near_ref, bf16[4,32,256]{2,1,0:T(8,128)(2,1)S(1)} %collective-permute-done.1.far_ref), custom_call_target="tpu_custom_call" | custom-call | tf_op jit(solution)/shard_map/pack/pallas_call | solution.py:62
  9.8 9.0 %all-to-all-start = ((bf16[32,40,256]{2,1,0:T(8,128)(2,1)}), bf16[32,40,256]{2,1,0:T(8,128)(2,1)S(1)}, u32[]{:S(2)}, u32[]{:S(2)}) async-start(bf16[32,40,256]{2,1,0:T(8,128)(2,1)} %pack.1), calls=%async_computation | async-start | bytes 1310720 | tf_op jit(solution)/shard_map/all_to_all | solution.py:356
  18.8 0.1 maximum_multiply_fusion.1
  18.9 2.5 %collective-permute-start.3 = (bf16[17,16,1024]{2,1,0:T(8,128)(2,1)S(1)}, bf16[17,16,1024]{2,1,0:T(8,128)(2,1)S(1)}, u32[]{:S(2)}, u32[]{:S(2)}) collective-permute-start(bf16[17,16,1024]{2,1,0:T(8,128)(2,1)S(1)} %maximum_multiply_fusion.1), channel_id=1, source_target_pairs={{1,2},{2,1},{5,6},{6,5},{9,10},{10,9},{13,14},{14,13},{17,18},{18,... | collective-permute-start | bytes 1671176 | tf_op jit(solution)/shard_map/ppermute | solution.py:357
  21.4 4.7 %bands.1 = (bf16[8,256,256]{2,1,0:T(8,128)(2,1)}, bf16[16,144,256]{2,1,0:T(8,128)(2,1)}, bf16[16,128,256]{2,1,0:T(8,128)(2,1)}, bf16[8,768,256]{2,1,0:T(8,128)(2,1)}) custom-call(bf16[16,21]{1,0:T(8,128)(2,1)} %row_ref.1, bf16[16,21]{1,0:T(8,128)(2,1)} %col_ref.1), custom_call_target="tpu_custom_call" | custom-call | tf_op jit(solution)/shard_map/bands/pallas_call | solution.py:116
  26.1 0.0 collective-permute-done.2.near_hbm
  26.1 7.5 %collective-permute-done.3.far_hbm = bf16[17,16,1024]{2,1,0:T(8,128)(2,1)S(1)} collective-permute-done((bf16[17,16,1024]{2,1,0:T(8,128)(2,1)S(1)}, bf16[17,16,1024]{2,1,0:T(8,128)(2,1)S(1)}, u32[]{:S(2)}, u32[]{:S(2)}) %collective-permute-start.3) | collective-permute-done | bytes 557088 | tf_op jit(solution)/shard_map/ppermute | solution.py:357
  33.6 0.0 all-to-all-done.strip_ref
  33.6 17.9 %main.1 = (f32[1,256,1024]{2,1,0:T(8,128)}, bf16[1024,256]{1,0:T(8,128)(2,1)}) custom-call(s32[1,1]{1,0:T(1,128)} %bitcast.1.even_ref, bf16[32,40,256]{2,1,0:T(8,128)(2,1)S(1)} %all-to-all-done.strip_ref, s32[1,256]{1,0:T(1,128)} %valid_ref.1, bf16[8,256,256]{2,1,0:T(8,128)(2,1)} %get-tuple-element.8.f_hbm, bf16[16,144,256]{2,1,0:T(8,128)(2,1)} %get-tuple-element.9.c_hbm, ...), custom_call_target="tpu_custom_call" | custom-call | tf_op jit(solution)/shard_map/main/pallas_call | solution.py:282
  51.5 18.8 %all_to_all.10.terms_ref = bf16[32,32,256]{2,1,0:T(8,128)(2,1)S(1)} all-to-all(bf16[32,32,256]{2,1,0:T(8,128)(2,1)} %bitcast.13), channel_id=1, replica_groups=mesh['exp'=32,'row'=4] {'exp'}, dimensions={0} | all-to-all | bytes 1048576 | tf_op jit(solution)/shard_map/all_to_all | solution.py:363
  70.3 1.5 %gather.1 = f32[4,32,256]{2,1,0:T(8,128)} custom-call(s32[1,32]{1,0:T(1,128)} %bitcast.19, bf16[32,32,256]{2,1,0:T(8,128)(2,1)S(1)} %all_to_all.10.terms_ref), custom_call_target="tpu_custom_call" | custom-call | tf_op jit(solution)/shard_map/gather/pallas_call | solution.py:323
Async XLA Ops:
  0.6 7.3 %collective-permute-start.1 = (bf16[4,32,256]{2,1,0:T(8,128)(2,1)}, bf16[4,32,256]{2,1,0:T(8,128)(2,1)S(1)}, u32[]{:S(2)}, u32[]{:S(2)}) collective-permute-start(bf16[4,32,256]{2,1,0:T(8,128)(2,1)} %bitcast.15), channel_id=1, source_target_pairs={{1,2},{2,1},{5,6},{6,5},{9,10},{10,9},{13,14},{14,13},{17,18},{18,... | collective-permute-start | bytes 196616 | tf_op jit(solution)/shard_map/ppermute | solution.py:350
  2.6 5.4 %collective-permute-start = (bf16[4,32,256]{2,1,0:T(8,128)(2,1)}, bf16[4,32,256]{2,1,0:T(8,128)(2,1)S(1)}, u32[]{:S(2)}, u32[]{:S(2)}) collective-permute-start(bf16[4,32,256]{2,1,0:T(8,128)(2,1)} %bitcast.16), channel_id=1, source_target_pairs={{0,1},{1,0},{2,3},{3,2},{4,5},{5,4},{6,7},{7,6},{8,9},{9,8},{10,11... | collective-permute-start | bytes 196616 | tf_op jit(solution)/shard_map/ppermute | solution.py:351
  5.6 20.5 %collective-permute-start.2 = (bf16[17,16,1024]{2,1,0:T(8,128)(2,1)S(1)}, bf16[17,16,1024]{2,1,0:T(8,128)(2,1)S(1)}, u32[]{:S(2)}, u32[]{:S(2)}) collective-permute-start(bf16[17,16,1024]{2,1,0:T(8,128)(2,1)S(1)} %maximum_multiply_fusion), channel_id=1, source_target_pairs={{0,1},{1,0},{2,3},{3,2},{4,5},{5,4},{6,7},{7,6},{8,9},{9,8},{10,11... | collective-permute-start | bytes 1671176 | tf_op jit(solution)/shard_map/ppermute | solution.py:358
  9.8 23.8 %all-to-all-start = ((bf16[32,40,256]{2,1,0:T(8,128)(2,1)}), bf16[32,40,256]{2,1,0:T(8,128)(2,1)S(1)}, u32[]{:S(2)}, u32[]{:S(2)}) async-start(bf16[32,40,256]{2,1,0:T(8,128)(2,1)} %pack.1), calls=%async_computation | async-start | bytes 1310720 | tf_op jit(solution)/shard_map/all_to_all | solution.py:356
  18.9 14.7 %collective-permute-start.3 = (bf16[17,16,1024]{2,1,0:T(8,128)(2,1)S(1)}, bf16[17,16,1024]{2,1,0:T(8,128)(2,1)S(1)}, u32[]{:S(2)}, u32[]{:S(2)}) collective-permute-start(bf16[17,16,1024]{2,1,0:T(8,128)(2,1)S(1)} %maximum_multiply_fusion.1), channel_id=1, source_target_pairs={{1,2},{2,1},{5,6},{6,5},{9,10},{10,9},{13,14},{14,13},{17,18},{18,... | collective-permute-start | bytes 1671176 | tf_op jit(solution)/shard_map/ppermute | solution.py:357

commit v3 on v2

--- a/solution.py
+++ b/solution.py
@@ -20,6 +20,9 @@
 OWN = COLS // EXPOSURES
 SKY = 24
 RIM = 16
+FULL = 8
+REST = HALF - FULL
+PLANES = KERNELS + 1
 LAT = ROWS + 2 * SKY
 EDGE = 8
 EXT = ROWS + 2 * RIM
@@ -40,6 +43,50 @@
 
 def column_of(valid):
     return jnp.broadcast_to(valid, (128, valid.shape[1])).T
+
+
+def cut_kernel(even_ref, valid_ref, obs_hbm, coef_hbm, near_ref, far_ref, near_in, far_in, sem):
+    even = even_ref[0, 0]
+    outs = ((even, near_ref, near_in), (1 - even, far_ref, far_in))
+    copies = []
+    for n, (last, _, block) in enumerate(outs):
+        rows = pl.ds(pl.multiple_of(last * (ROWS - RIM), RIM), RIM)
+        copies += [
+            pltpu.make_async_copy(coef_hbm.at[0, :, rows, :], block.at[pl.ds(0, KERNELS)], sem.at[2 * n]),
+            pltpu.make_async_copy(obs_hbm.at[0, rows, :], block.at[KERNELS], sem.at[2 * n + 1]),
+        ]
+    for copy in copies:
+        copy.start()
+    mask = column_of(valid_ref[...].astype(F32))
+    head_mask = jnp.concatenate([mask[:RIM]] * BLOCKS, axis=1)
+    tail_mask = jnp.concatenate([mask[ROWS - RIM :]] * BLOCKS, axis=1)
+    for copy in copies:
+        copy.wait()
+    for last, out, block in outs:
+        tail = last > 0
+        usable = jnp.where(tail, tail_mask, head_mask)
+        rest = []
+        for k in range(PLANES):
+            rows = block[k].astype(F32) * usable
+            out[k] = jnp.where(tail, rows[RIM - FULL :], rows[:FULL]).astype(BF16)
+            rest.append(jnp.where(tail, rows[RIM - HALF : RIM - FULL], rows[FULL:HALF]))
+        rest += [jnp.zeros((REST, COLS), F32)] * (-PLANES * REST % FULL // REST)
+        for n in range(len(rest) * REST // FULL):
+            each = FULL // REST
+            out[PLANES + n] = jnp.concatenate(rest[each * n : each * n + each], axis=0).astype(BF16)
+
+
+def cut(even, valid, observed, coefficients):
+    planes = PLANES + -(-PLANES * REST // FULL)
+    block = pltpu.VMEM((PLANES, RIM, COLS), BF16)
+    return pl.pallas_call(
+        cut_kernel,
+        out_shape=(jax.ShapeDtypeStruct((planes, FULL, COLS), BF16),) * 2,
+        in_specs=[SMEM, VMEM, HBM, HBM],
+        out_specs=(VMEM,) * 2,
+        scratch_shapes=[block, block, pltpu.SemaphoreType.DMA((4,))],
+        name="cut",
+    )(even, valid, observed, coefficients)
 
 
 def pack_kernel(even_ref, cell_ref, lat_ref, near_ref, far_ref, out_ref, turned):
@@ -135,7 +182,7 @@
 
 
 def main_kernel(
-    even_ref, strip_ref, valid_ref, f_hbm, c_hbm, a_hbm, b_hbm, coef_hbm, obs_hbm, near_hbm, far_hbm,
+    even_ref, strip_ref, valid_ref, f_hbm, c_hbm, a_hbm, b_hbm, coef_hbm, obs_hbm, near_ref, far_ref,
     res_hbm, send_ref,
     f_ref, c_ref, a_ref, b_ref, sky, windows, coef, obs, rb, rb2, pred, w, w2, cb, cb2, acc, sem, rim_sem, band_sem,
 ):
@@ -143,14 +190,14 @@
         return pltpu.make_async_copy(coef_hbm.at[0, k], coef.at[k, pl.ds(RIM, ROWS), :], sem.at[k])
 
     even = even_ref[0, 0]
-    near_at = pl.ds(pl.multiple_of(even * (RIM + ROWS), RIM), RIM)
-    far_at = pl.ds(pl.multiple_of((1 - even) * (RIM + ROWS), RIM), RIM)
+    near_at = pl.ds(pl.multiple_of(FULL + even * (FULL + ROWS), FULL), FULL)
+    far_at = pl.ds(pl.multiple_of(FULL + (1 - even) * (FULL + ROWS), FULL), FULL)
     rims_in = [
         pltpu.make_async_copy(obs_hbm.at[0], obs.at[pl.ds(RIM, ROWS), :], rim_sem.at[0]),
-        pltpu.make_async_copy(near_hbm.at[KERNELS], obs.at[near_at, :], rim_sem.at[1]),
-        pltpu.make_async_copy(far_hbm.at[KERNELS], obs.at[far_at, :], rim_sem.at[2]),
-        pltpu.make_async_copy(near_hbm.at[pl.ds(0, KERNELS)], coef.at[:, near_at, :], rim_sem.at[3]),
-        pltpu.make_async_copy(far_hbm.at[pl.ds(0, KERNELS)], coef.at[:, far_at, :], rim_sem.at[4]),
+        pltpu.make_async_copy(near_ref.at[KERNELS], obs.at[near_at, :], rim_sem.at[1]),
+        pltpu.make_async_copy(far_ref.at[KERNELS], obs.at[far_at, :], rim_sem.at[2]),
+        pltpu.make_async_copy(near_ref.at[pl.ds(0, KERNELS)], coef.at[:, near_at, :], rim_sem.at[3]),
+        pltpu.make_async_copy(far_ref.at[pl.ds(0, KERNELS)], coef.at[:, far_at, :], rim_sem.at[4]),
     ]
     f_in = pltpu.make_async_copy(f_hbm, f_ref, band_sem.at[3])
     c_in = pltpu.make_async_copy(c_hbm, c_ref, band_sem.at[2])
@@ -173,6 +220,21 @@
     for r in (w, w2):
         r[:, :, EXT:, :] = jnp.zeros((2, BLOCKS, WR - EXT, 128), BF16)
     acc[...] = jnp.zeros_like(acc)
+    none = jnp.zeros((FULL - REST, COLS), F32)
+    for k in range(PLANES):
+        plane, at = PLANES + REST * k // FULL, REST * k % FULL
+        near_rest = near_ref[plane].astype(F32)[at : at + REST]
+        far_rest = far_ref[plane].astype(F32)[at : at + REST]
+        rest_above = jnp.where(even > 0, far_rest, near_rest)
+        rest_below = jnp.where(even > 0, near_rest, far_rest)
+        tile_above = jnp.concatenate([none, rest_above], axis=0).astype(BF16)
+        tile_below = jnp.concatenate([rest_below, none], axis=0).astype(BF16)
+        if k < KERNELS:
+            coef[k, 0:FULL, :] = tile_above
+            coef[k, EXT - FULL :, :] = tile_below
+        else:
+            obs[0:FULL, :] = tile_above
+            obs[EXT - FULL :, :] = tile_below
     low = lax.broadcasted_iota(jnp.int32, (LAT, 128), 1) < 64
     for j in range(BLOCKS):
         own, edges = [], []
@@ -341,17 +403,10 @@
     cell_of = cell_of.reshape(1, EXPOSURES)
     latent = jnp.swapaxes(latent, 1, 2)
 
-    def rim(start):
-        coef = lax.dynamic_slice_in_dim(coefficients[0], start, RIM, 1)
-        seen = lax.dynamic_slice_in_dim(observed, start, RIM, 1)
-        usable = lax.dynamic_slice_in_dim(valid_rows[0], start, RIM, 0).astype(BF16)
-        return jnp.concatenate([coef, seen], axis=0) * usable[None, :, None]
-
+    even = even.reshape(1, 1)
     far_sky = lax.ppermute(latent, "row", across)
     near_sky = lax.ppermute(latent, "row", chip)
-    far_rim = rim((1 - even) * (ROWS - RIM))
-    near_rim = rim(even * (ROWS - RIM))
-    even = even.reshape(1, 1)
+    near_rim, far_rim = cut(even, valid_rows, observed, coefficients)
     packed = pack(even, cell_of, latent, *keep(near_sky, far_sky))
     strip = lax.all_to_all(packed, "exp", 0, 0, tiled=True)
     far_rim = lax.ppermute(far_rim, "row", across)

time: 72.3 us -> 70.6 us (0.976)
  the two profiles are of different devices: /device:TPU:4 before, /device:TPU:1 now
where the time goes in v3:
time: 70.6 us; the launch traced here: 69.3 us
  Pallas kernels  29.1 us (41%)
  starting transfers between devices  20.3 us (29%)
  blocking collectives  16.6 us (24%)
  waiting for transfers between devices  2.63 us (4%)
  between operations  0.71 us (1%)
    pallas_call x1, Pallas kernels, main(): pl.pallas_call(main_kernel, out_shape=(jax.ShapeDtypeStruct((1, ROWS, COL...  17.9 us
    all_to_all x1, blocking collectives, body(): lax.all_to_all(send.reshape(EXPOSURES, OWN, ROWS), 'exp', 0, 0, tiled=True)  16.6 us
    all_to_all x1, starting transfers between devices, body(): strip = lax.all_to_all(packed, 'exp', 0, 0, tiled=True)  8.92 us
    ppermute x1, starting transfers between devices, body(): far_sky = lax.ppermute(latent, 'row', across)  6.03 us
    ppermute x1, starting transfers between devices, body(): far_rim = lax.ppermute(far_rim, 'row', across)  5.2 us
    pallas_call x1, Pallas kernels, make_bands(): pl.pallas_call(bands_kernel, out_shape=(jax.ShapeDtypeStruct((PAIRS, 256,...  4.72 us
    pallas_call x1, Pallas kernels, cut(): pl.pallas_call(cut_kernel, out_shape=(jax.ShapeDtypeStruct((planes, FULL,...  3.02 us
    ppermute x1, waiting for transfers between devices, body(): far_sky = lax.ppermute(latent, 'row', across)  2.05 us
  transfers between devices with their start and end apart: 5, of which 2 were waited for; matrix products, arithmetic and copies ran while one was open for 0% of the time, Pallas kernels for 11%

profile of v3, /device:TPU:1, one launch (start us, length us, event | category | flops | bytes accessed | tf_op | source)
XLA Modules:
  0.0 69.3 jit_solution(4294632948688312191)
XLA Ops:
  0.6 6.0 %collective-permute-start.1 = (bf16[4,32,256]{2,1,0:T(8,128)(2,1)}, bf16[4,32,256]{2,1,0:T(8,128)(2,1)S(1)}, u32[]{:S(2)}, u32[]{:S(2)}) collective-permute-start(bf16[4,32,256]{2,1,0:T(8,128)(2,1)} %bitcast.7), channel_id=1, source_target_pairs={{1,2},{2,1},{5,6},{6,5},{9,10},{10,9},{13,14},{14,13},{17,18},{18,... | collective-permute-start | bytes 196616 | tf_op jit(solution)/shard_map/ppermute | solution.py:407
  6.7 0.1 collective-permute-start
  6.8 2.0 %collective-permute-done.1.far_ref = bf16[4,32,256]{2,1,0:T(8,128)(2,1)S(1)} collective-permute-done((bf16[4,32,256]{2,1,0:T(8,128)(2,1)}, bf16[4,32,256]{2,1,0:T(8,128)(2,1)S(1)}, u32[]{:S(2)}, u32[]{:S(2)}) %collective-permute-start.1) | collective-permute-done | bytes 65568 | tf_op jit(solution)/shard_map/ppermute | solution.py:407
  8.8 0.0 collective-permute-done.near_ref
  8.8 1.9 %pack.1 = bf16[32,40,256]{2,1,0:T(8,128)(2,1)} custom-call(s32[1,1]{1,0:T(1,128)} %bitcast.1.even_ref, s32[1,32]{1,0:T(1,128)} %bitcast.10, bf16[4,32,256]{2,1,0:T(8,128)(2,1)} %bitcast.9, bf16[4,32,256]{2,1,0:T(8,128)(2,1)S(1)} %collective-permute-done.near_ref, bf16[4,32,256]{2,1,0:T(8,128)(2,1)S(1)} %collective-permute-done.1.far_ref), custom_call_target="tpu_custom_call" | custom-call | tf_op jit(solution)/shard_map/pack/pallas_call | solution.py:109
  10.7 8.9 %all-to-all-start = ((bf16[32,40,256]{2,1,0:T(8,128)(2,1)}), bf16[32,40,256]{2,1,0:T(8,128)(2,1)S(1)}, u32[]{:S(2)}, u32[]{:S(2)}) async-start(bf16[32,40,256]{2,1,0:T(8,128)(2,1)} %pack.1), calls=%async_computation | async-start | bytes 1310720 | tf_op jit(solution)/shard_map/all_to_all | solution.py:411
  19.6 3.0 %cut.1 = (bf16[22,8,1024]{2,1,0:T(8,128)(2,1)}, bf16[22,8,1024]{2,1,0:T(8,128)(2,1)}) custom-call(s32[1,1]{1,0:T(1,128)} %bitcast.1.even_ref, s32[1,256]{1,0:T(1,128)} %valid_ref.3, bf16[1,256,1024]{2,1,0:T(8,128)(2,1)} %obs_hbm.3, bf16[1,16,256,1024]{3,2,1,0:T(8,128)(2,1)} %coef_hbm.3), custom_call_target="tpu_custom_call" | custom-call | tf_op jit(solution)/shard_map/cut/pallas_call | solution.py:82
  22.6 0.1 collective-permute-start.2
  22.7 5.2 %collective-permute-start.3 = (bf16[22,8,1024]{2,1,0:T(8,128)(2,1)}, bf16[22,8,1024]{2,1,0:T(8,128)(2,1)S(1)}, u32[]{:S(2)}, u32[]{:S(2)}) collective-permute-start(bf16[22,8,1024]{2,1,0:T(8,128)(2,1)} %get-tuple-element.15), channel_id=1, source_target_pairs={{1,2},{2,1},{5,6},{6,5},{9,10},{10,9},{13,14},{14,13},{17,18},{18,... | collective-permute-start | bytes 1081352 | tf_op jit(solution)/shard_map/ppermute | solution.py:412
  27.9 4.7 %bands.1 = (bf16[8,256,256]{2,1,0:T(8,128)(2,1)}, bf16[16,144,256]{2,1,0:T(8,128)(2,1)}, bf16[16,128,256]{2,1,0:T(8,128)(2,1)}, bf16[8,768,256]{2,1,0:T(8,128)(2,1)}) custom-call(bf16[16,21]{1,0:T(8,128)(2,1)} %row_ref.1, bf16[16,21]{1,0:T(8,128)(2,1)} %col_ref.1), custom_call_target="tpu_custom_call" | custom-call | tf_op jit(solution)/shard_map/bands/pallas_call | solution.py:163
  32.7 0.0 collective-permute-done.2.near_ref
  32.7 0.6 collective-permute-done.3.far_ref
  33.3 0.0 all-to-all-done.strip_ref
  33.3 17.9 %main.1 = (f32[1,256,1024]{2,1,0:T(8,128)}, bf16[1024,256]{1,0:T(8,128)(2,1)}) custom-call(s32[1,1]{1,0:T(1,128)} %bitcast.1.even_ref, bf16[32,40,256]{2,1,0:T(8,128)(2,1)S(1)} %all-to-all-done.strip_ref, s32[1,256]{1,0:T(1,128)} %valid_ref.3, bf16[8,256,256]{2,1,0:T(8,128)(2,1)} %get-tuple-element.10.f_hbm, bf16[16,144,256]{2,1,0:T(8,128)(2,1)} %get-tuple-element.11.c_hbm, ...), custom_call_target="tpu_custom_call" | custom-call | tf_op jit(solution)/shard_map/main/pallas_call | solution.py:344
  51.2 16.6 %all_to_all.10.terms_ref = bf16[32,32,256]{2,1,0:T(8,128)(2,1)S(1)} all-to-all(bf16[32,32,256]{2,1,0:T(8,128)(2,1)} %bitcast.5), channel_id=1, replica_groups=mesh['exp'=32,'row'=4] {'exp'}, dimensions={0} | all-to-all | bytes 1048576 | tf_op jit(solution)/shard_map/all_to_all | solution.py:418
  67.7 1.5 %gather.1 = f32[4,32,256]{2,1,0:T(8,128)} custom-call(s32[1,32]{1,0:T(1,128)} %bitcast.11, bf16[32,32,256]{2,1,0:T(8,128)(2,1)S(1)} %all_to_all.10.terms_ref), custom_call_target="tpu_custom_call" | custom-call | tf_op jit(solution)/shard_map/gather/pallas_call | solution.py:385
Async XLA Ops:
  0.6 8.2 %collective-permute-start.1 = (bf16[4,32,256]{2,1,0:T(8,128)(2,1)}, bf16[4,32,256]{2,1,0:T(8,128)(2,1)S(1)}, u32[]{:S(2)}, u32[]{:S(2)}) collective-permute-start(bf16[4,32,256]{2,1,0:T(8,128)(2,1)} %bitcast.7), channel_id=1, source_target_pairs={{1,2},{2,1},{5,6},{6,5},{9,10},{10,9},{13,14},{14,13},{17,18},{18,... | collective-permute-start | bytes 196616 | tf_op jit(solution)/shard_map/ppermute | solution.py:407
  6.7 2.1 %collective-permute-start = (bf16[4,32,256]{2,1,0:T(8,128)(2,1)}, bf16[4,32,256]{2,1,0:T(8,128)(2,1)S(1)}, u32[]{:S(2)}, u32[]{:S(2)}) collective-permute-start(bf16[4,32,256]{2,1,0:T(8,128)(2,1)} %bitcast.8), channel_id=1, source_target_pairs={{0,1},{1,0},{2,3},{3,2},{4,5},{5,4},{6,7},{7,6},{8,9},{9,8},{10,11... | collective-permute-start | bytes 196616 | tf_op jit(solution)/shard_map/ppermute | solution.py:408
  10.7 22.6 %all-to-all-start = ((bf16[32,40,256]{2,1,0:T(8,128)(2,1)}), bf16[32,40,256]{2,1,0:T(8,128)(2,1)S(1)}, u32[]{:S(2)}, u32[]{:S(2)}) async-start(bf16[32,40,256]{2,1,0:T(8,128)(2,1)} %pack.1), calls=%async_computation | async-start | bytes 1310720 | tf_op jit(solution)/shard_map/all_to_all | solution.py:411
  22.6 10.0 %collective-permute-start.2 = (bf16[22,8,1024]{2,1,0:T(8,128)(2,1)}, bf16[22,8,1024]{2,1,0:T(8,128)(2,1)S(1)}, u32[]{:S(2)}, u32[]{:S(2)}) collective-permute-start(bf16[22,8,1024]{2,1,0:T(8,128)(2,1)} %get-tuple-element.14), channel_id=1, source_target_pairs={{0,1},{1,0},{2,3},{3,2},{4,5},{5,4},{6,7},{7,6},{8,9},{9,8},{10,11... | collective-permute-start | bytes 1081352 | tf_op jit(solution)/shard_map/ppermute | solution.py:413
  22.7 10.5 %collective-permute-start.3 = (bf16[22,8,1024]{2,1,0:T(8,128)(2,1)}, bf16[22,8,1024]{2,1,0:T(8,128)(2,1)S(1)}, u32[]{:S(2)}, u32[]{:S(2)}) collective-permute-start(bf16[22,8,1024]{2,1,0:T(8,128)(2,1)} %get-tuple-element.15), channel_id=1, source_target_pairs={{1,2},{2,1},{5,6},{6,5},{9,10},{10,9},{13,14},{14,13},{17,18},{18,... | collective-permute-start | bytes 1081352 | tf_op jit(solution)/shard_map/ppermute | solution.py:412

commit v4 on v3

--- a/solution.py
+++ b/solution.py
@@ -203,9 +203,9 @@
     c_in = pltpu.make_async_copy(c_hbm, c_ref, band_sem.at[2])
     a_in = pltpu.make_async_copy(a_hbm, a_ref, band_sem.at[0])
     b_in = pltpu.make_async_copy(b_hbm, b_ref, band_sem.at[1])
+    f_in.start()
     for copy in rims_in[:3]:
         copy.start()
-    f_in.start()
     c_in.start()
     for copy in rims_in[3:]:
         copy.start()
@@ -252,13 +252,6 @@
         before = sky[j - 1] if j > 0 else zero
         windows[j, :, 0:128] = sky[j].astype(BF16)
         windows[j, :, 128:256] = jnp.where(low, after, before).astype(BF16)
-    for copy in rims_in[:3]:
-        copy.wait()
-    pred[...] = -obs[...].astype(F32)
-    for copy in rims_in[3:]:
-        copy.wait()
-    f_in.wait()
-    c_in.wait()
 
     def blur(i, rb):
         f = f_ref[i]
@@ -288,7 +281,20 @@
         predict(2 * n + 1, rb2)
         return carry
 
-    lax.fori_loop(0, PAIRS // 2, forward, 0)
+    f_in.wait()
+    blur(0, rb)
+    blur(1, rb2)
+    for copy in rims_in[:3]:
+        copy.wait()
+    pred[...] = -obs[...].astype(F32)
+    for copy in rims_in[3:]:
+        copy.wait()
+    c_in.wait()
+    for m in range(4):
+        coef_in(m).wait()
+    predict(0, rb)
+    predict(1, rb2)
+    lax.fori_loop(1, PAIRS // 2, forward, 0)
 
     mask = column_of(valid_ref[...].astype(F32))
     for j in range(BLOCKS):

time: 70.6 us -> 70.2 us (level)
  no operation moved by 1% of the time
where the time goes in v4:
time: 70.2 us; the launch traced here: 68.9 us
  Pallas kernels  28.7 us (41%)
  starting transfers between devices  20.3 us (29%)
  blocking collectives  16.6 us (24%)
  waiting for transfers between devices  2.63 us (4%)
  between operations  0.71 us (1%)
    pallas_call x1, Pallas kernels, main(): pl.pallas_call(main_kernel, out_shape=(jax.ShapeDtypeStruct((1, ROWS, COL...  17.5 us
    all_to_all x1, blocking collectives, body(): lax.all_to_all(send.reshape(EXPOSURES, OWN, ROWS), 'exp', 0, 0, tiled=True)  16.6 us
    all_to_all x1, starting transfers between devices, body(): strip = lax.all_to_all(packed, 'exp', 0, 0, tiled=True)  8.92 us
    ppermute x1, starting transfers between devices, body(): far_sky = lax.ppermute(latent, 'row', across)  6.03 us
    ppermute x1, starting transfers between devices, body(): far_rim = lax.ppermute(far_rim, 'row', across)  5.2 us
    pallas_call x1, Pallas kernels, make_bands(): pl.pallas_call(bands_kernel, out_shape=(jax.ShapeDtypeStruct((PAIRS, 256,...  4.72 us
    pallas_call x1, Pallas kernels, cut(): pl.pallas_call(cut_kernel, out_shape=(jax.ShapeDtypeStruct((planes, FULL,...  3.02 us
    ppermute x1, waiting for transfers between devices, body(): far_sky = lax.ppermute(latent, 'row', across)  2.05 us
  transfers between devices with their start and end apart: 5, of which 2 were waited for; matrix products, arithmetic and copies ran while one was open for 0% of the time, Pallas kernels for 11%

profile of v4, /device:TPU:1, one launch (start us, length us, event | category | flops | bytes accessed | tf_op | source)
XLA Modules:
  0.0 68.9 jit_solution(7637194539662890079)
XLA Ops:
  0.6 6.0 %collective-permute-start.1 = (bf16[4,32,256]{2,1,0:T(8,128)(2,1)}, bf16[4,32,256]{2,1,0:T(8,128)(2,1)S(1)}, u32[]{:S(2)}, u32[]{:S(2)}) collective-permute-start(bf16[4,32,256]{2,1,0:T(8,128)(2,1)} %bitcast.7), channel_id=1, source_target_pairs={{1,2},{2,1},{5,6},{6,5},{9,10},{10,9},{13,14},{14,13},{17,18},{18,... | collective-permute-start | bytes 196616 | tf_op jit(solution)/shard_map/ppermute | solution.py:413
  6.7 0.1 collective-permute-start
  6.8 2.0 %collective-permute-done.1.far_ref = bf16[4,32,256]{2,1,0:T(8,128)(2,1)S(1)} collective-permute-done((bf16[4,32,256]{2,1,0:T(8,128)(2,1)}, bf16[4,32,256]{2,1,0:T(8,128)(2,1)S(1)}, u32[]{:S(2)}, u32[]{:S(2)}) %collective-permute-start.1) | collective-permute-done | bytes 65568 | tf_op jit(solution)/shard_map/ppermute | solution.py:413
  8.8 0.0 collective-permute-done.near_ref
  8.8 1.9 %pack.1 = bf16[32,40,256]{2,1,0:T(8,128)(2,1)} custom-call(s32[1,1]{1,0:T(1,128)} %bitcast.1.even_ref, s32[1,32]{1,0:T(1,128)} %bitcast.10, bf16[4,32,256]{2,1,0:T(8,128)(2,1)} %bitcast.9, bf16[4,32,256]{2,1,0:T(8,128)(2,1)S(1)} %collective-permute-done.near_ref, bf16[4,32,256]{2,1,0:T(8,128)(2,1)S(1)} %collective-permute-done.1.far_ref), custom_call_target="tpu_custom_call" | custom-call | tf_op jit(solution)/shard_map/pack/pallas_call | solution.py:109
  10.7 8.9 %all-to-all-start = ((bf16[32,40,256]{2,1,0:T(8,128)(2,1)}), bf16[32,40,256]{2,1,0:T(8,128)(2,1)S(1)}, u32[]{:S(2)}, u32[]{:S(2)}) async-start(bf16[32,40,256]{2,1,0:T(8,128)(2,1)} %pack.1), calls=%async_computation | async-start | bytes 1310720 | tf_op jit(solution)/shard_map/all_to_all | solution.py:417
  19.6 3.0 %cut.1 = (bf16[22,8,1024]{2,1,0:T(8,128)(2,1)}, bf16[22,8,1024]{2,1,0:T(8,128)(2,1)}) custom-call(s32[1,1]{1,0:T(1,128)} %bitcast.1.even_ref, s32[1,256]{1,0:T(1,128)} %valid_ref.3, bf16[1,256,1024]{2,1,0:T(8,128)(2,1)} %obs_hbm.3, bf16[1,16,256,1024]{3,2,1,0:T(8,128)(2,1)} %coef_hbm.3), custom_call_target="tpu_custom_call" | custom-call | tf_op jit(solution)/shard_map/cut/pallas_call | solution.py:82
  22.6 0.1 collective-permute-start.2
  22.7 5.2 %collective-permute-start.3 = (bf16[22,8,1024]{2,1,0:T(8,128)(2,1)}, bf16[22,8,1024]{2,1,0:T(8,128)(2,1)S(1)}, u32[]{:S(2)}, u32[]{:S(2)}) collective-permute-start(bf16[22,8,1024]{2,1,0:T(8,128)(2,1)} %get-tuple-element.15), channel_id=1, source_target_pairs={{1,2},{2,1},{5,6},{6,5},{9,10},{10,9},{13,14},{14,13},{17,18},{18,... | collective-permute-start | bytes 1081352 | tf_op jit(solution)/shard_map/ppermute | solution.py:418
  27.9 4.7 %bands.1 = (bf16[8,256,256]{2,1,0:T(8,128)(2,1)}, bf16[16,144,256]{2,1,0:T(8,128)(2,1)}, bf16[16,128,256]{2,1,0:T(8,128)(2,1)}, bf16[8,768,256]{2,1,0:T(8,128)(2,1)}) custom-call(bf16[16,21]{1,0:T(8,128)(2,1)} %row_ref.1, bf16[16,21]{1,0:T(8,128)(2,1)} %col_ref.1), custom_call_target="tpu_custom_call" | custom-call | tf_op jit(solution)/shard_map/bands/pallas_call | solution.py:163
  32.7 0.0 collective-permute-done.2.near_ref
  32.7 0.6 collective-permute-done.3.far_ref
  33.3 0.0 all-to-all-done.strip_ref
  33.3 17.5 %main.1 = (f32[1,256,1024]{2,1,0:T(8,128)}, bf16[1024,256]{1,0:T(8,128)(2,1)}) custom-call(s32[1,1]{1,0:T(1,128)} %bitcast.1.even_ref, bf16[32,40,256]{2,1,0:T(8,128)(2,1)S(1)} %all-to-all-done.strip_ref, s32[1,256]{1,0:T(1,128)} %valid_ref.3, bf16[8,256,256]{2,1,0:T(8,128)(2,1)} %get-tuple-element.10.f_hbm, bf16[16,144,256]{2,1,0:T(8,128)(2,1)} %get-tuple-element.11.c_hbm, ...), custom_call_target="tpu_custom_call" | custom-call | tf_op jit(solution)/shard_map/main/pallas_call | solution.py:350
  50.8 16.6 %all_to_all.10.terms_ref = bf16[32,32,256]{2,1,0:T(8,128)(2,1)S(1)} all-to-all(bf16[32,32,256]{2,1,0:T(8,128)(2,1)} %bitcast.5), channel_id=1, replica_groups=mesh['exp'=32,'row'=4] {'exp'}, dimensions={0} | all-to-all | bytes 1048576 | tf_op jit(solution)/shard_map/all_to_all | solution.py:424
  67.4 1.5 %gather.1 = f32[4,32,256]{2,1,0:T(8,128)} custom-call(s32[1,32]{1,0:T(1,128)} %bitcast.11, bf16[32,32,256]{2,1,0:T(8,128)(2,1)S(1)} %all_to_all.10.terms_ref), custom_call_target="tpu_custom_call" | custom-call | tf_op jit(solution)/shard_map/gather/pallas_call | solution.py:391
Async XLA Ops:
  0.6 8.2 %collective-permute-start.1 = (bf16[4,32,256]{2,1,0:T(8,128)(2,1)}, bf16[4,32,256]{2,1,0:T(8,128)(2,1)S(1)}, u32[]{:S(2)}, u32[]{:S(2)}) collective-permute-start(bf16[4,32,256]{2,1,0:T(8,128)(2,1)} %bitcast.7), channel_id=1, source_target_pairs={{1,2},{2,1},{5,6},{6,5},{9,10},{10,9},{13,14},{14,13},{17,18},{18,... | collective-permute-start | bytes 196616 | tf_op jit(solution)/shard_map/ppermute | solution.py:413
  6.7 2.1 %collective-permute-start = (bf16[4,32,256]{2,1,0:T(8,128)(2,1)}, bf16[4,32,256]{2,1,0:T(8,128)(2,1)S(1)}, u32[]{:S(2)}, u32[]{:S(2)}) collective-permute-start(bf16[4,32,256]{2,1,0:T(8,128)(2,1)} %bitcast.8), channel_id=1, source_target_pairs={{0,1},{1,0},{2,3},{3,2},{4,5},{5,4},{6,7},{7,6},{8,9},{9,8},{10,11... | collective-permute-start | bytes 196616 | tf_op jit(solution)/shard_map/ppermute | solution.py:414
  10.7 22.6 %all-to-all-start = ((bf16[32,40,256]{2,1,0:T(8,128)(2,1)}), bf16[32,40,256]{2,1,0:T(8,128)(2,1)S(1)}, u32[]{:S(2)}, u32[]{:S(2)}) async-start(bf16[32,40,256]{2,1,0:T(8,128)(2,1)} %pack.1), calls=%async_computation | async-start | bytes 1310720 | tf_op jit(solution)/shard_map/all_to_all | solution.py:417
  22.6 10.0 %collective-permute-start.2 = (bf16[22,8,1024]{2,1,0:T(8,128)(2,1)}, bf16[22,8,1024]{2,1,0:T(8,128)(2,1)S(1)}, u32[]{:S(2)}, u32[]{:S(2)}) collective-permute-start(bf16[22,8,1024]{2,1,0:T(8,128)(2,1)} %get-tuple-element.14), channel_id=1, source_target_pairs={{0,1},{1,0},{2,3},{3,2},{4,5},{5,4},{6,7},{7,6},{8,9},{9,8},{10,11... | collective-permute-start | bytes 1081352 | tf_op jit(solution)/shard_map/ppermute | solution.py:419
  22.7 10.5 %collective-permute-start.3 = (bf16[22,8,1024]{2,1,0:T(8,128)(2,1)}, bf16[22,8,1024]{2,1,0:T(8,128)(2,1)S(1)}, u32[]{:S(2)}, u32[]{:S(2)}) collective-permute-start(bf16[22,8,1024]{2,1,0:T(8,128)(2,1)} %get-tuple-element.15), channel_id=1, source_target_pairs={{1,2},{2,1},{5,6},{6,5},{9,10},{10,9},{13,14},{14,13},{17,18},{18,... | collective-permute-start | bytes 1081352 | tf_op jit(solution)/shard_map/ppermute | solution.py:418

commit v5 on v4

--- a/solution.py
+++ b/solution.py
@@ -45,51 +45,63 @@
     return jnp.broadcast_to(valid, (128, valid.shape[1])).T
 
 
-def cut_kernel(even_ref, valid_ref, obs_hbm, coef_hbm, near_ref, far_ref, near_in, far_in, sem):
+def cut_kernel(even_ref, valid_ref, obs_hbm, coef_hbm, near_hbm, far_hbm, blocks, made, sem, out_sem):
     even = even_ref[0, 0]
-    outs = ((even, near_ref, near_in), (1 - even, far_ref, far_in))
-    copies = []
-    for n, (last, _, block) in enumerate(outs):
+    lasts = (1 - even, even)
+    copies, outs = [], []
+    for n, (last, target) in enumerate(zip(lasts, (far_hbm, near_hbm))):
         rows = pl.ds(pl.multiple_of(last * (ROWS - RIM), RIM), RIM)
-        copies += [
-            pltpu.make_async_copy(coef_hbm.at[0, :, rows, :], block.at[pl.ds(0, KERNELS)], sem.at[2 * n]),
-            pltpu.make_async_copy(obs_hbm.at[0, rows, :], block.at[KERNELS], sem.at[2 * n + 1]),
-        ]
-    for copy in copies:
+        copies.append(
+            [
+                pltpu.make_async_copy(
+                    coef_hbm.at[0, :, rows, :], blocks.at[n, pl.ds(0, KERNELS)], sem.at[2 * n]
+                ),
+                pltpu.make_async_copy(obs_hbm.at[0, rows, :], blocks.at[n, KERNELS], sem.at[2 * n + 1]),
+            ]
+        )
+        outs.append(pltpu.make_async_copy(made.at[n], target, out_sem.at[n]))
+    for copy in copies[0] + copies[1]:
         copy.start()
     mask = column_of(valid_ref[...].astype(F32))
     head_mask = jnp.concatenate([mask[:RIM]] * BLOCKS, axis=1)
     tail_mask = jnp.concatenate([mask[ROWS - RIM :]] * BLOCKS, axis=1)
-    for copy in copies:
-        copy.wait()
-    for last, out, block in outs:
+    for n, last in enumerate(lasts):
+        for copy in copies[n]:
+            copy.wait()
         tail = last > 0
         usable = jnp.where(tail, tail_mask, head_mask)
         rest = []
         for k in range(PLANES):
-            rows = block[k].astype(F32) * usable
-            out[k] = jnp.where(tail, rows[RIM - FULL :], rows[:FULL]).astype(BF16)
+            rows = blocks[n, k].astype(F32) * usable
+            made[n, k] = jnp.where(tail, rows[RIM - FULL :], rows[:FULL]).astype(BF16)
             rest.append(jnp.where(tail, rows[RIM - HALF : RIM - FULL], rows[FULL:HALF]))
         rest += [jnp.zeros((REST, COLS), F32)] * (-PLANES * REST % FULL // REST)
-        for n in range(len(rest) * REST // FULL):
+        for m in range(len(rest) * REST // FULL):
             each = FULL // REST
-            out[PLANES + n] = jnp.concatenate(rest[each * n : each * n + each], axis=0).astype(BF16)
+            made[n, PLANES + m] = jnp.concatenate(rest[each * m : each * m + each], axis=0).astype(BF16)
+        outs[n].start()
+    for copy in outs:
+        copy.wait()
 
 
 def cut(even, valid, observed, coefficients):
     planes = PLANES + -(-PLANES * REST // FULL)
-    block = pltpu.VMEM((PLANES, RIM, COLS), BF16)
     return pl.pallas_call(
         cut_kernel,
         out_shape=(jax.ShapeDtypeStruct((planes, FULL, COLS), BF16),) * 2,
         in_specs=[SMEM, VMEM, HBM, HBM],
-        out_specs=(VMEM,) * 2,
-        scratch_shapes=[block, block, pltpu.SemaphoreType.DMA((4,))],
+        out_specs=(HBM,) * 2,
+        scratch_shapes=[
+            pltpu.VMEM((2, PLANES, RIM, COLS), BF16),
+            pltpu.VMEM((2, planes, FULL, COLS), BF16),
+            pltpu.SemaphoreType.DMA((4,)),
+            pltpu.SemaphoreType.DMA((2,)),
+        ],
         name="cut",
     )(even, valid, observed, coefficients)
 
 
-def pack_kernel(even_ref, cell_ref, lat_ref, near_ref, far_ref, out_ref, turned):
+def pack_kernel(even_ref, cell_ref, lat_ref, near_ref, far_ref, out_hbm, turned, sem):
     even = even_ref[0, 0] > 0
     fill = jnp.zeros((OWN, 64 - 2 * SKY), F32)
     for c in range(CELLS):
@@ -101,8 +113,13 @@
         turned[c, OWN:, :] = jnp.concatenate(
             [edges[EDGE * g : EDGE * g + EDGE] for g in range(OWN // EDGE)], axis=1
         ).astype(BF16)
-    for e in range(EXPOSURES):
-        out_ref[e] = turned[cell_ref[0, e]]
+    copies = [
+        pltpu.make_async_copy(turned.at[cell_ref[0, e]], out_hbm.at[e], sem.at[e]) for e in range(EXPOSURES)
+    ]
+    for copy in copies:
+        copy.start()
+    for copy in copies:
+        copy.wait()
 
 
 def pack(even, cell_of, latent, near, far):
@@ -110,8 +127,8 @@
         pack_kernel,
         out_shape=jax.ShapeDtypeStruct((EXPOSURES, OWN + EDGE, ROWS), BF16),
         in_specs=[SMEM, SMEM, VMEM, VMEM, VMEM],
-        out_specs=VMEM,
-        scratch_shapes=[pltpu.VMEM((CELLS, OWN + EDGE, ROWS), BF16)],
+        out_specs=HBM,
+        scratch_shapes=[pltpu.VMEM((CELLS, OWN + EDGE, ROWS), BF16), pltpu.SemaphoreType.DMA((EXPOSURES,))],
         name="pack",
     )(even, cell_of, latent, near, far)
 
@@ -183,8 +200,8 @@
 
 def main_kernel(
     even_ref, strip_ref, valid_ref, f_hbm, c_hbm, a_hbm, b_hbm, coef_hbm, obs_hbm, near_ref, far_ref,
-    res_hbm, send_ref,
-    f_ref, c_ref, a_ref, b_ref, sky, windows, coef, obs, rb, rb2, pred, w, w2, cb, cb2, acc, sem, rim_sem, band_sem,
+    res_hbm, send_hbm,
+    f_ref, c_ref, a_ref, b_ref, turned, sky, windows, coef, obs, rb, rb2, pred, w, w2, cb, cb2, acc, sem, rim_sem, band_sem,
 ):
     def coef_in(k):
         return pltpu.make_async_copy(coef_hbm.at[0, k], coef.at[k, pl.ds(RIM, ROWS), :], sem.at[k])
@@ -341,9 +358,14 @@
         return carry
 
     lax.fori_loop(0, PAIRS // 2, adjoint, 0)
+    outs = []
     for x in range(BLOCKS // 2):
-        send_ref[256 * x : 256 * x + 256, :] = acc[x].T.astype(BF16)
-    res_out.wait()
+        at = pl.ds(256 * x, 256)
+        turned[at, :] = acc[x].T.astype(BF16)
+        outs.append(pltpu.make_async_copy(turned.at[at, :], send_hbm.at[at, :], rim_sem.at[1 + x]))
+        outs[x].start()
+    for copy in (*outs, res_out):
+        copy.wait()
 
 
 def main(even, strip, valid, bands, coefficients, observed, near, far):
@@ -354,12 +376,13 @@
             jax.ShapeDtypeStruct((COLS, ROWS), BF16),
         ),
         in_specs=[SMEM] + [VMEM] * 2 + [HBM] * 6 + [VMEM] * 2,
-        out_specs=(ANY, VMEM),
+        out_specs=(HBM, HBM),
         scratch_shapes=[
             pltpu.VMEM((PAIRS, 256, 256), BF16),
             pltpu.VMEM((KERNELS, HOUT, 256), BF16),
             pltpu.VMEM((KERNELS, 128, 256), BF16),
             pltpu.VMEM((PAIRS, 768, 256), BF16),
+            pltpu.VMEM((COLS, ROWS), BF16),
             pltpu.VMEM((BLOCKS, LAT, 128), F32),
             pltpu.VMEM((BLOCKS, LAT, 256), BF16),
             pltpu.VMEM((KERNELS, EXT, COLS), BF16),

time: 70.2 us -> 70.2 us (level)
  no operation moved by 1% of the time
where the time goes in v5:
time: 70.2 us; the launch traced here: 68.9 us
  Pallas kernels  28.6 us (41%)
  starting transfers between devices  20.3 us (29%)
  blocking collectives  16.6 us (24%)
  waiting for transfers between devices  2.63 us (4%)
  between operations  0.72 us (1%)
    pallas_call x1, Pallas kernels, main(): pl.pallas_call(main_kernel, out_shape=(jax.ShapeDtypeStruct((1, ROWS, COL...  17.4 us
    all_to_all x1, blocking collectives, body(): lax.all_to_all(send.reshape(EXPOSURES, OWN, ROWS), 'exp', 0, 0, tiled=True)  16.6 us
    all_to_all x1, starting transfers between devices, body(): strip = lax.all_to_all(packed, 'exp', 0, 0, tiled=True)  8.93 us
    ppermute x1, starting transfers between devices, body(): far_sky = lax.ppermute(latent, 'row', across)  6.03 us
    ppermute x1, starting transfers between devices, body(): far_rim = lax.ppermute(far_rim, 'row', across)  5.2 us
    pallas_call x1, Pallas kernels, make_bands(): pl.pallas_call(bands_kernel, out_shape=(jax.ShapeDtypeStruct((PAIRS, 256,...  4.72 us
    pallas_call x1, Pallas kernels, cut(): pl.pallas_call(cut_kernel, out_shape=(jax.ShapeDtypeStruct((planes, FULL,...  2.89 us
    pallas_call x1, Pallas kernels, pack(): pl.pallas_call(pack_kernel, out_shape=jax.ShapeDtypeStruct((EXPOSURES, OW...  2.09 us
  transfers between devices with their start and end apart: 5, of which 2 were waited for; matrix products, arithmetic and copies ran while one was open for 0% of the time, Pallas kernels for 11%

profile of v5, /device:TPU:1, one launch (start us, length us, event | category | flops | bytes accessed | tf_op | source)
XLA Modules:
  0.0 68.9 jit_solution(12816215352177245888)
XLA Ops:
  0.6 6.0 %collective-permute-start.1 = (bf16[4,32,256]{2,1,0:T(8,128)(2,1)}, bf16[4,32,256]{2,1,0:T(8,128)(2,1)S(1)}, u32[]{:S(2)}, u32[]{:S(2)}) collective-permute-start(bf16[4,32,256]{2,1,0:T(8,128)(2,1)} %bitcast.7), channel_id=1, source_target_pairs={{1,2},{2,1},{5,6},{6,5},{9,10},{10,9},{13,14},{14,13},{17,18},{18,... | collective-permute-start | bytes 196616 | tf_op jit(solution)/shard_map/ppermute | solution.py:436
  6.7 0.1 collective-permute-start
  6.8 2.0 %collective-permute-done.1.far_ref = bf16[4,32,256]{2,1,0:T(8,128)(2,1)S(1)} collective-permute-done((bf16[4,32,256]{2,1,0:T(8,128)(2,1)}, bf16[4,32,256]{2,1,0:T(8,128)(2,1)S(1)}, u32[]{:S(2)}, u32[]{:S(2)}) %collective-permute-start.1) | collective-permute-done | bytes 65568 | tf_op jit(solution)/shard_map/ppermute | solution.py:436
  8.8 0.0 collective-permute-done.near_ref
  8.8 2.1 %pack.1 = bf16[32,40,256]{2,1,0:T(8,128)(2,1)} custom-call(s32[1,1]{1,0:T(1,128)} %bitcast.1.even_ref, s32[1,32]{1,0:T(1,128)} %bitcast.10, bf16[4,32,256]{2,1,0:T(8,128)(2,1)} %bitcast.9, bf16[4,32,256]{2,1,0:T(8,128)(2,1)S(1)} %collective-permute-done.near_ref, bf16[4,32,256]{2,1,0:T(8,128)(2,1)S(1)} %collective-permute-done.1.far_ref), custom_call_target="tpu_custom_call" | custom-call | tf_op jit(solution)/shard_map/pack/pallas_call | solution.py:126
  10.9 8.9 %all-to-all-start = ((bf16[32,40,256]{2,1,0:T(8,128)(2,1)}), bf16[32,40,256]{2,1,0:T(8,128)(2,1)S(1)}, u32[]{:S(2)}, u32[]{:S(2)}) async-start(bf16[32,40,256]{2,1,0:T(8,128)(2,1)} %pack.1), calls=%async_computation | async-start | bytes 1310720 | tf_op jit(solution)/shard_map/all_to_all | solution.py:440
  19.8 2.9 %cut.1 = (bf16[22,8,1024]{2,1,0:T(8,128)(2,1)}, bf16[22,8,1024]{2,1,0:T(8,128)(2,1)}) custom-call(s32[1,1]{1,0:T(1,128)} %bitcast.1.even_ref, s32[1,256]{1,0:T(1,128)} %valid_ref.3, bf16[1,256,1024]{2,1,0:T(8,128)(2,1)} %obs_hbm.3, bf16[1,16,256,1024]{3,2,1,0:T(8,128)(2,1)} %coef_hbm.3), custom_call_target="tpu_custom_call" | custom-call | tf_op jit(solution)/shard_map/cut/pallas_call | solution.py:89
  22.7 0.1 collective-permute-start.2
  22.8 5.2 %collective-permute-start.3 = (bf16[22,8,1024]{2,1,0:T(8,128)(2,1)}, bf16[22,8,1024]{2,1,0:T(8,128)(2,1)S(1)}, u32[]{:S(2)}, u32[]{:S(2)}) collective-permute-start(bf16[22,8,1024]{2,1,0:T(8,128)(2,1)} %get-tuple-element.15), channel_id=1, source_target_pairs={{1,2},{2,1},{5,6},{6,5},{9,10},{10,9},{13,14},{14,13},{17,18},{18,... | collective-permute-start | bytes 1081352 | tf_op jit(solution)/shard_map/ppermute | solution.py:441
  28.0 4.7 %bands.1 = (bf16[8,256,256]{2,1,0:T(8,128)(2,1)}, bf16[16,144,256]{2,1,0:T(8,128)(2,1)}, bf16[16,128,256]{2,1,0:T(8,128)(2,1)}, bf16[8,768,256]{2,1,0:T(8,128)(2,1)}) custom-call(bf16[16,21]{1,0:T(8,128)(2,1)} %row_ref.1, bf16[16,21]{1,0:T(8,128)(2,1)} %col_ref.1), custom_call_target="tpu_custom_call" | custom-call | tf_op jit(solution)/shard_map/bands/pallas_call | solution.py:180
  32.8 0.0 collective-permute-done.2.near_ref
  32.8 0.6 collective-permute-done.3.far_ref
  33.3 0.0 all-to-all-done.strip_ref
  33.3 17.4 %main.1 = (f32[1,256,1024]{2,1,0:T(8,128)}, bf16[1024,256]{1,0:T(8,128)(2,1)}) custom-call(s32[1,1]{1,0:T(1,128)} %bitcast.1.even_ref, bf16[32,40,256]{2,1,0:T(8,128)(2,1)S(1)} %all-to-all-done.strip_ref, s32[1,256]{1,0:T(1,128)} %valid_ref.3, bf16[8,256,256]{2,1,0:T(8,128)(2,1)} %get-tuple-element.10.f_hbm, bf16[16,144,256]{2,1,0:T(8,128)(2,1)} %get-tuple-element.11.c_hbm, ...), custom_call_target="tpu_custom_call" | custom-call | tf_op jit(solution)/shard_map/main/pallas_call | solution.py:372
  50.8 16.6 %all_to_all.10.terms_ref = bf16[32,32,256]{2,1,0:T(8,128)(2,1)S(1)} all-to-all(bf16[32,32,256]{2,1,0:T(8,128)(2,1)} %bitcast.5), channel_id=1, replica_groups=mesh['exp'=32,'row'=4] {'exp'}, dimensions={0} | all-to-all | bytes 1048576 | tf_op jit(solution)/shard_map/all_to_all | solution.py:447
  67.3 1.5 %gather.1 = f32[4,32,256]{2,1,0:T(8,128)} custom-call(s32[1,32]{1,0:T(1,128)} %bitcast.11, bf16[32,32,256]{2,1,0:T(8,128)(2,1)S(1)} %all_to_all.10.terms_ref), custom_call_target="tpu_custom_call" | custom-call | tf_op jit(solution)/shard_map/gather/pallas_call | solution.py:414
Async XLA Ops:
  0.6 8.2 %collective-permute-start.1 = (bf16[4,32,256]{2,1,0:T(8,128)(2,1)}, bf16[4,32,256]{2,1,0:T(8,128)(2,1)S(1)}, u32[]{:S(2)}, u32[]{:S(2)}) collective-permute-start(bf16[4,32,256]{2,1,0:T(8,128)(2,1)} %bitcast.7), channel_id=1, source_target_pairs={{1,2},{2,1},{5,6},{6,5},{9,10},{10,9},{13,14},{14,13},{17,18},{18,... | collective-permute-start | bytes 196616 | tf_op jit(solution)/shard_map/ppermute | solution.py:436
  6.7 2.1 %collective-permute-start = (bf16[4,32,256]{2,1,0:T(8,128)(2,1)}, bf16[4,32,256]{2,1,0:T(8,128)(2,1)S(1)}, u32[]{:S(2)}, u32[]{:S(2)}) collective-permute-start(bf16[4,32,256]{2,1,0:T(8,128)(2,1)} %bitcast.8), channel_id=1, source_target_pairs={{0,1},{1,0},{2,3},{3,2},{4,5},{5,4},{6,7},{7,6},{8,9},{9,8},{10,11... | collective-permute-start | bytes 196616 | tf_op jit(solution)/shard_map/ppermute | solution.py:437
  10.9 22.4 %all-to-all-start = ((bf16[32,40,256]{2,1,0:T(8,128)(2,1)}), bf16[32,40,256]{2,1,0:T(8,128)(2,1)S(1)}, u32[]{:S(2)}, u32[]{:S(2)}) async-start(bf16[32,40,256]{2,1,0:T(8,128)(2,1)} %pack.1), calls=%async_computation | async-start | bytes 1310720 | tf_op jit(solution)/shard_map/all_to_all | solution.py:440
  22.7 10.0 %collective-permute-start.2 = (bf16[22,8,1024]{2,1,0:T(8,128)(2,1)}, bf16[22,8,1024]{2,1,0:T(8,128)(2,1)S(1)}, u32[]{:S(2)}, u32[]{:S(2)}) collective-permute-start(bf16[22,8,1024]{2,1,0:T(8,128)(2,1)} %get-tuple-element.14), channel_id=1, source_target_pairs={{0,1},{1,0},{2,3},{3,2},{4,5},{5,4},{6,7},{7,6},{8,9},{9,8},{10,11... | collective-permute-start | bytes 1081352 | tf_op jit(solution)/shard_map/ppermute | solution.py:442
  22.8 10.5 %collective-permute-start.3 = (bf16[22,8,1024]{2,1,0:T(8,128)(2,1)}, bf16[22,8,1024]{2,1,0:T(8,128)(2,1)S(1)}, u32[]{:S(2)}, u32[]{:S(2)}) collective-permute-start(bf16[22,8,1024]{2,1,0:T(8,128)(2,1)} %get-tuple-element.15), channel_id=1, source_target_pairs={{1,2},{2,1},{5,6},{6,5},{9,10},{10,9},{13,14},{14,13},{17,18},{18,... | collective-permute-start | bytes 1081352 | tf_op jit(solution)/shard_map/ppermute | solution.py:441
